TPU v7x, 32 devices: a whole 2x2x4 slice. The times are simulated.
32 devices in a mesh: grp: 2 (over y), dev: 16 (over z, x, core).
Axes of the slice: x: 2, y: 2, z: 4, core: 2. Of those that a mesh axis runs over, the one named last changes fastest.
Arguments:
- queries: float32 [128, 1024], P(('grp', 'dev')), may hold values from -4.5 to 4.5
- documents: float32 [4096, 1024], P(('grp', 'dev')), may hold values from -0.75 to 0.75
- doc_codes: int32 [4096, 128], P(('grp', 'dev')), may hold values from 0 to 255
- codebook: float32 [256, 1024], replicated, may hold values from -0.75 to 0.75
- candidate_owner: int32 [128, 32], P(('grp', 'dev')), may hold values from 0 to 31, all different within a row; in each aligned block of 4 rows (0 to 3, 4 to 7, ...) at most 4 rows name the same one
- candidate_local: int32 [128, 32], P(('grp', 'dev')), may hold values from 0 to 127
Outputs:
- codebook_gradient: float32 [256, 1024], P('dev', 'grp')
- query_loss: float32 [128], P(('grp', 'dev'))
Inputs may be any that keep to these rules, and one draw needn't show every extreme that they name: `candidate_owner`: each query names 32 different owners; among one device's 4 queries no owner is named more than 4 times, and in some device's queries one owner is named exactly 4 times.
All inputs are finite; a program needn't handle non-finite values.
Results may differ from a plain program's by a relative error of at most 0.0003.
Values sent between devices are 32-bit elements; how exact they have to be, the bound alone decides.
No kernel may reach another device: no remote copies, remote signals or barrier semaphores. Data moves between devices by JAX's collectives and lax.ppermute only.
A program may use at most 192 MiB of HBM per device.

v0:
```python
import jax
import jax.numpy as jnp
from jax import lax
from jax.sharding import PartitionSpec as P

D = 1024
M = 128
K = 256
C = 32
SUB = 8


def slot_positions(candidate_owner, capacity):
    owner_flat = candidate_owner.reshape(-1)
    ordinal = jnp.arange(owner_flat.shape[0], dtype=jnp.int32)
    earlier = (owner_flat[None, :] == owner_flat[:, None]) & (ordinal[None, :] < ordinal[:, None])
    rank_inside = jnp.sum(earlier.astype(jnp.int32), axis=1)
    return owner_flat * capacity + rank_inside


def distill(exact_score, student):
    teacher = jax.nn.softmax(exact_score, axis=-1)
    query_loss = jnp.sum(
        teacher * (jax.nn.log_softmax(exact_score, axis=-1) - jax.nn.log_softmax(student, axis=-1)),
        axis=-1,
    )
    weight = jax.nn.softmax(student, axis=-1) - teacher
    return (query_loss, weight)


def code_onehot(code_block):
    return (code_block[:, :, None] == jnp.arange(K, dtype=jnp.int32)[None, None, :]).astype(
        jnp.float32
    )


def fetched_terms(queries, vectors, code_rows, codebook):
    query_count = queries.shape[0]
    exact_score = jnp.einsum("qcd,qd->qc", vectors, queries, precision=lax.Precision.HIGHEST)
    query_parts = queries.reshape(query_count, M, SUB)
    lookup = jnp.einsum(
        "qmj,kmj->qmk", query_parts, codebook.reshape(K, M, SUB), precision=lax.Precision.HIGHEST
    )

    def student_one(pieces):
        code_one, lookup_one = pieces
        return jnp.einsum(
            "cmk,mk->c", code_onehot(code_one), lookup_one, precision=lax.Precision.HIGHEST
        )

    student = lax.map(student_one, (code_rows, lookup))
    query_loss, weight = distill(exact_score, student)

    def table_one(pieces):
        code_one, weight_one = pieces
        return jnp.einsum(
            "cmk,c->mk", code_onehot(code_one), weight_one, precision=lax.Precision.HIGHEST
        )

    weight_table = lax.map(table_one, (code_rows, weight))
    gradient = jnp.einsum(
        "qmk,qmj->kmj", weight_table, query_parts, precision=lax.Precision.HIGHEST
    )
    return (query_loss, gradient.reshape(K, D))


def shards(queries, documents, doc_codes, codebook, candidate_owner, candidate_local):
    groups = lax.axis_size("grp")
    owners = lax.axis_size("dev")
    query_count = queries.shape[0]
    capacity = min(query_count, max(2, 2 * query_count * C // (groups * owners)))
    slot_count = groups * owners * capacity
    positions = slot_positions(candidate_owner, capacity)
    wanted = jnp.zeros((slot_count,), jnp.int32).at[positions].set(candidate_local.reshape(-1))
    asked = lax.all_to_all(
        lax.all_to_all(
            wanted.reshape(groups, owners, capacity), "grp", split_axis=0, concat_axis=0, tiled=True
        ),
        "dev",
        split_axis=1,
        concat_axis=1,
        tiled=True,
    )
    doc_index = asked.reshape(slot_count)
    found_rows = documents[doc_index].reshape(groups, owners, capacity, D)
    found_codes = doc_codes[doc_index].astype(jnp.float32).reshape(groups, owners, capacity, M)
    fetched, fetched_codes = (
        lax.all_to_all(
            lax.all_to_all(found_rows, "grp", split_axis=0, concat_axis=0, tiled=True),
            "dev",
            split_axis=1,
            concat_axis=1,
            tiled=True,
        ),
        lax.all_to_all(
            lax.all_to_all(found_codes, "grp", split_axis=0, concat_axis=0, tiled=True),
            "dev",
            split_axis=1,
            concat_axis=1,
            tiled=True,
        ),
    )
    vectors = fetched.reshape(slot_count, D)[positions].reshape(query_count, C, D)
    code_rows = (
        fetched_codes.reshape(slot_count, M)[positions].astype(jnp.int32).reshape(query_count, C, M)
    )
    query_loss, local_gradient = fetched_terms(queries, vectors, code_rows, codebook)
    partial_sum = lax.psum_scatter(local_gradient, "dev", scatter_dimension=0, tiled=True)
    codebook_gradient = lax.psum_scatter(partial_sum, "grp", scatter_dimension=1, tiled=True)
    return (codebook_gradient, query_loss)


def solution(mesh):
    in_specs = (
        P(("grp", "dev"), None),
        P(("grp", "dev"), None),
        P(("grp", "dev"), None),
        P(),
        P(("grp", "dev"), None),
        P(("grp", "dev"), None),
    )
    out_specs = (P("dev", "grp"), P(("grp", "dev")))
    return jax.shard_map(shards, mesh=mesh, in_specs=in_specs, out_specs=out_specs, check_vma=False)
```

profile of v0, /device:TPU:0, one launch (start us, length us, event | category | flops | bytes accessed | tf_op | source)
XLA Modules:
  0.0 180.2 jit_solution(6461381742338682574)
XLA Ops:
  7.2 0.8 broadcast_multiply_fusion
  8.0 0.8 eq.45
  8.8 0.1 mul.21
  8.8 0.2 convert_reduce_fusion
  9.0 0.8 reshape.158
  9.8 1.0 scatter_custom_fusion
  10.8 0.1 reshape.113
  10.9 0.1 copy.46
  11.0 7.8 %all_to_all.30 = s32[2,16,4]{1,2,0:T(4,128)S(1)} all-to-all(s32[2,16,4]{1,2,0:T(4,128)S(1)} %copy.46), channel_id=1, replica_groups=mesh['grp'=2,'dev'=16] {'grp'}, dimensions={0} | all-to-all | bytes 1024 | tf_op jit(solution)/shard_map/all_to_all | solution.py:76
  18.8 0.1 copy.47
  18.9 12.2 %all_to_all.31 = s32[2,16,4]{2,0,1:T(2,128)S(1)} all-to-all(s32[2,16,4]{2,0,1:T(2,128)S(1)} %copy.47), channel_id=1, replica_groups=mesh['grp'=2,'dev'=16] {'dev'}, dimensions={1} | all-to-all | bytes 1024 | tf_op jit(solution)/shard_map/all_to_all | solution.py:75
  31.1 0.1 reshape.114
  31.2 1.5 gather_fusion
  32.7 6.5 %all_to_all.32 = f32[2,16,4,128]{3,2,1,0:T(4,128)S(1)} all-to-all(f32[2,16,4,128]{3,2,1,0:T(4,128)S(1)} %bitcast.63), channel_id=1, replica_groups=mesh['grp'=2,'dev'=16] {'grp'}, dimensions={0} | all-to-all | bytes 131072 | tf_op jit(solution)/shard_map/all_to_all | solution.py:96
  39.2 0.6 copy.49
  39.8 3.5 %all-to-all-start.3 = ((f32[2,16,4,128]{3,2,0,1:T(4,128)}), f32[2,16,4,128]{3,2,0,1:T(4,128)S(1)}, u32[]{:S(2)}, u32[]{:S(2)}) async-start(f32[2,16,4,128]{3,2,0,1:T(4,128)} %copy.49), calls=%async_computation.3 | async-start | bytes 131072 | tf_op jit(solution)/shard_map/all_to_all | solution.py:95
  43.4 0.2 reshape.117
  43.5 0.3 copy.51
  43.9 0.8 gather_fusion.2
  44.7 1.0 reshape.118
  45.7 4.5 %all-to-all-done.3 = f32[2,16,4,128]{3,2,0,1:T(4,128)S(1)} async-done(((f32[2,16,4,128]{3,2,0,1:T(4,128)}), f32[2,16,4,128]{3,2,0,1:T(4,128)S(1)}, u32[]{:S(2)}, u32[]{:S(2)}) %all-to-all-start.3) | async-done | bytes 65568 | tf_op jit(solution)/shard_map/all_to_all | solution.py:95
  50.2 3.5 %all-to-all-start.4 = ((f32[2,16,4,1024]{3,2,1,0:T(4,128)}), f32[2,16,4,1024]{3,2,1,0:T(4,128)S(1)}, u32[]{:S(2)}, u32[]{:S(2)}) async-start(f32[2,16,4,1024]{3,2,1,0:T(4,128)} %reshape.118), calls=%async_computation.4 | async-start | bytes 1048576 | tf_op jit(solution)/shard_map/all_to_all | solution.py:89
  53.7 1.1 convolution_bitcast_fusion.1
  54.9 0.6 gather_fusion.1
  55.5 6.1 %all-to-all-done.4 = f32[2,16,4,1024]{3,2,1,0:T(4,128)S(1)} async-done(((f32[2,16,4,1024]{3,2,1,0:T(4,128)}), f32[2,16,4,1024]{3,2,1,0:T(4,128)S(1)}, u32[]{:S(2)}, u32[]{:S(2)}) %all-to-all-start.4) | async-done | bytes 524320 | tf_op jit(solution)/shard_map/all_to_all | solution.py:89
  61.7 0.9 copy.54
  62.5 3.6 %all-to-all-start.5 = ((f32[2,16,4,1024]{3,2,0,1:T(4,128)}), f32[2,16,4,1024]{3,2,0,1:T(4,128)S(1)}, u32[]{:S(2)}, u32[]{:S(2)}) async-start(f32[2,16,4,1024]{3,2,0,1:T(4,128)} %copy.54), calls=%async_computation.5 | async-start | bytes 1048576 | tf_op jit(solution)/shard_map/all_to_all | solution.py:88
  66.1 0.0 reduce-scatter.3.cloned.1.call-start
  66.1 6.7 %while.20 = (s32[]{:T(128)}, f32[4,32]{1,0:T(4,128)S(1)}, s32[4,32,128]{2,1,0:T(8,128)S(1)}, f32[4,128,256]{2,0,1:T(4,128)S(1)}, s32[]{:T(128)}, /*index=5*/s32[]{:T(128)}) while((s32[]{:T(128)}, f32[4,32]{1,0:T(4,128)S(1)}, s32[4,32,128]{2,1,0:T(8,128)S(1)}, f32[4,128,256]{2,0,1:T(4,128)S(1)}, s32[]{:T(128)}, /*index=5*/s32[]{:T(128)}) %tuple.53), condition=%wide.region_3.4_spmd, body=%wide.region_2.3_spmd.sunk | while | flops 3145698 | bytes 704977 | solution.py:51
  66.2 0.1 constant_dynamic-slice_fusion.2
  66.3 1.5 select_reduce_fusion.2
  67.8 0.1 constant_dynamic-slice_fusion.2
  68.0 1.5 select_reduce_fusion.2
  69.5 0.1 constant_dynamic-slice_fusion.2
  69.7 1.5 select_reduce_fusion.2
  71.2 0.1 constant_dynamic-slice_fusion.2
  71.4 1.5 select_reduce_fusion.2
  72.9 0.1 reduce_max.27
  73.0 7.5 %all-to-all-done.5 = f32[2,16,4,1024]{3,2,0,1:T(4,128)S(1)} async-done(((f32[2,16,4,1024]{3,2,0,1:T(4,128)}), f32[2,16,4,1024]{3,2,0,1:T(4,128)S(1)}, u32[]{:S(2)}, u32[]{:S(2)}) %all-to-all-start.5) | async-done | bytes 524320 | tf_op jit(solution)/shard_map/all_to_all | solution.py:88
  80.6 0.2 reshape.119
  80.8 0.8 gather_fusion.3
  81.6 0.6 fusion.8
  82.1 0.1 reduce_max.28
  82.2 0.2 exponential_reduce_fusion
  82.5 0.7 fusion.11
  83.2 19.7 %while.21 = (s32[]{:T(128)}, f32[4,128,256]{2,0,1:T(4,128)S(1)}, s32[4,32,128]{2,1,0:T(8,128)S(1)}, f32[4,32]{1,0:T(4,128)S(1)}, s32[]{:T(128)}, /*index=5*/s32[]{:T(128)}) while((s32[]{:T(128)}, f32[4,128,256]{2,0,1:T(4,128)S(1)}, s32[4,32,128]{2,1,0:T(8,128)S(1)}, f32[4,32]{1,0:T(4,128)S(1)}, s32[]{:T(128)}, /*index=5*/s32[]{:T(128)}) %tuple.55), condition=%wide.region_9.10_spmd, body=%wide.region_8.9_spmd.sunk | while | flops 13631490 | bytes 2540113 | solution.py:60
  83.2 0.8 iota_compare_fusion.4
  84.1 2.2 %fusion.21 = f32[1,128,256]{2,0,1:T(1,128)S(1)} fusion(pred[32,128,256]{2,1,0:T(32,128)(4,1)S(1)} %iota_compare_fusion.4, f32[4,32]{1,0:T(4,128)S(1)} %get-tuple-element.172, s32[]{:T(128)} %get-tuple-element.163), kind=kOutput, calls=%fused_computation.6.clone.1 | convolution fusion | flops 12582912 | bytes 1180164 | tf_op jit(solution)/shard_map/while/body/eval_jaxpr/cmk,c->mk/dot_general | solution.py:56
  86.2 1.8 %dynamic_update_slice.11 = f32[4,128,256]{2,0,1:T(4,128)S(1)} dynamic-update-slice(f32[4,128,256]{2,0,1:T(4,128)S(1)} %get-tuple-element.164, f32[1,128,256]{2,0,1:T(1,128)S(1)} %fusion.21, s32[]{:T(128)} %get-tuple-element.163, s32[]{:T(128)} %constant.21.clone.1..sunk.1, s32[]{:T(128)} %constant.21.clone.1..sunk.1) | dynamic-update-slice | bytes 262148 | tf_op jit(solution)/shard_map/while/body/jit(dynamic_update_index_in_dim)/dynamic_update_slice | solution.py:60
  88.1 0.9 iota_compare_fusion.4
  89.0 2.2 %fusion.21 = f32[1,128,256]{2,0,1:T(1,128)S(1)} fusion(pred[32,128,256]{2,1,0:T(32,128)(4,1)S(1)} %iota_compare_fusion.4, f32[4,32]{1,0:T(4,128)S(1)} %get-tuple-element.172, s32[]{:T(128)} %get-tuple-element.163), kind=kOutput, calls=%fused_computation.6.clone.1 | convolution fusion | flops 12582912 | bytes 1180164 | tf_op jit(solution)/shard_map/while/body/eval_jaxpr/cmk,c->mk/dot_general | solution.py:56
  91.2 1.8 %dynamic_update_slice.11 = f32[4,128,256]{2,0,1:T(4,128)S(1)} dynamic-update-slice(f32[4,128,256]{2,0,1:T(4,128)S(1)} %get-tuple-element.164, f32[1,128,256]{2,0,1:T(1,128)S(1)} %fusion.21, s32[]{:T(128)} %get-tuple-element.163, s32[]{:T(128)} %constant.21.clone.1..sunk.1, s32[]{:T(128)} %constant.21.clone.1..sunk.1) | dynamic-update-slice | bytes 262148 | tf_op jit(solution)/shard_map/while/body/jit(dynamic_update_index_in_dim)/dynamic_update_slice | solution.py:60
  93.1 0.9 iota_compare_fusion.4
  93.9 2.2 %fusion.21 = f32[1,128,256]{2,0,1:T(1,128)S(1)} fusion(pred[32,128,256]{2,1,0:T(32,128)(4,1)S(1)} %iota_compare_fusion.4, f32[4,32]{1,0:T(4,128)S(1)} %get-tuple-element.172, s32[]{:T(128)} %get-tuple-element.163), kind=kOutput, calls=%fused_computation.6.clone.1 | convolution fusion | flops 12582912 | bytes 1180164 | tf_op jit(solution)/shard_map/while/body/eval_jaxpr/cmk,c->mk/dot_general | solution.py:56
  96.1 1.8 %dynamic_update_slice.11 = f32[4,128,256]{2,0,1:T(4,128)S(1)} dynamic-update-slice(f32[4,128,256]{2,0,1:T(4,128)S(1)} %get-tuple-element.164, f32[1,128,256]{2,0,1:T(1,128)S(1)} %fusion.21, s32[]{:T(128)} %get-tuple-element.163, s32[]{:T(128)} %constant.21.clone.1..sunk.1, s32[]{:T(128)} %constant.21.clone.1..sunk.1) | dynamic-update-slice | bytes 262148 | tf_op jit(solution)/shard_map/while/body/jit(dynamic_update_index_in_dim)/dynamic_update_slice | solution.py:60
  98.0 0.9 iota_compare_fusion.4
  98.9 2.2 %fusion.21 = f32[1,128,256]{2,0,1:T(1,128)S(1)} fusion(pred[32,128,256]{2,1,0:T(32,128)(4,1)S(1)} %iota_compare_fusion.4, f32[4,32]{1,0:T(4,128)S(1)} %get-tuple-element.172, s32[]{:T(128)} %get-tuple-element.163), kind=kOutput, calls=%fused_computation.6.clone.1 | convolution fusion | flops 12582912 | bytes 1180164 | tf_op jit(solution)/shard_map/while/body/eval_jaxpr/cmk,c->mk/dot_general | solution.py:56
  101.0 1.8 %dynamic_update_slice.11 = f32[4,128,256]{2,0,1:T(4,128)S(1)} dynamic-update-slice(f32[4,128,256]{2,0,1:T(4,128)S(1)} %get-tuple-element.164, f32[1,128,256]{2,0,1:T(1,128)S(1)} %fusion.21, s32[]{:T(128)} %get-tuple-element.163, s32[]{:T(128)} %constant.21.clone.1..sunk.1, s32[]{:T(128)} %constant.21.clone.1..sunk.1) | dynamic-update-slice | bytes 262148 | tf_op jit(solution)/shard_map/while/body/jit(dynamic_update_index_in_dim)/dynamic_update_slice | solution.py:60
  102.9 1.4 convolution_bitcast_fusion
  104.3 1.3 copy.58
  105.6 0.0 reduce-scatter.3.cloned.1.call-update
  105.6 0.0 reduce-scatter.5.cloned.1.call-start
  105.7 55.9 %reduce-scatter.3.cloned.1.call-done = f32[16,1024]{1,0:T(8,128)} async-done(((f32[256,1024]{1,0:T(8,128)}), f32[16,1024]{1,0:T(8,128)}) %reduce-scatter.3.cloned.1.call-update) | async-done | bytes 65552 | tf_op jit(solution)/shard_map/reduce_scatter | solution.py:108
  161.6 11.7 %reduce-scatter.5.cloned.1.call-done = f32[16,512]{1,0:T(8,128)} async-done(((f32[16,1024]{1,0:T(8,128)}), f32[16,512]{1,0:T(8,128)}) %reduce-scatter.5.cloned.1.call-update) | async-done | bytes 32784 | tf_op jit(solution)/shard_map/reduce_scatter | solution.py:109
  (38 shorter events, 0.4 us)
Async XLA Ops:
  7.2 36.7 %copy-start = (f32[128,1024]{1,0:T(8,128)S(1)}, f32[128,1024]{1,0:T(8,128)}, u32[]{:S(2)}) copy-start(f32[128,1024]{1,0:T(8,128)} %param.12) | copy-start | bytes 1572868
  7.2 36.2 %copy-start.3 = (f32[4,1024]{1,0:T(4,128)S(1)}, f32[4,1024]{1,0:T(4,128)}, u32[]{:S(2)}) copy-start(f32[4,1024]{1,0:T(4,128)} %param.11) | copy-start | bytes 49156
  7.2 36.4 %copy-start.1 = (f32[256,1024]{1,0:T(8,128)S(1)}, f32[256,1024]{1,0:T(8,128)}, u32[]{:S(2)}) copy-start(f32[256,1024]{1,0:T(8,128)} %param.14) | copy-start | bytes 3145732
  39.8 10.4 %all-to-all-start.3 = ((f32[2,16,4,128]{3,2,0,1:T(4,128)}), f32[2,16,4,128]{3,2,0,1:T(4,128)S(1)}, u32[]{:S(2)}, u32[]{:S(2)}) async-start(f32[2,16,4,128]{3,2,0,1:T(4,128)} %copy.49), calls=%async_computation.3 | async-start | bytes 131072 | tf_op jit(solution)/shard_map/all_to_all | solution.py:95
  50.2 11.5 %all-to-all-start.4 = ((f32[2,16,4,1024]{3,2,1,0:T(4,128)}), f32[2,16,4,1024]{3,2,1,0:T(4,128)S(1)}, u32[]{:S(2)}, u32[]{:S(2)}) async-start(f32[2,16,4,1024]{3,2,1,0:T(4,128)} %reshape.118), calls=%async_computation.4 | async-start | bytes 1048576 | tf_op jit(solution)/shard_map/all_to_all | solution.py:89
  62.5 18.0 %all-to-all-start.5 = ((f32[2,16,4,1024]{3,2,0,1:T(4,128)}), f32[2,16,4,1024]{3,2,0,1:T(4,128)S(1)}, u32[]{:S(2)}, u32[]{:S(2)}) async-start(f32[2,16,4,1024]{3,2,0,1:T(4,128)} %copy.54), calls=%async_computation.5 | async-start | bytes 1048576 | tf_op jit(solution)/shard_map/all_to_all | solution.py:88
  66.1 95.5 %reduce-scatter.3.cloned.1.call-start = ((), (), s32[]{:S(2)}) async-start(), calls=%async_computation.8 | async-start | bytes 1114112 | tf_op jit(solution)/shard_map/reduce_scatter | solution.py:108
  80.7 2.5 %copy-start.2 = (f32[4,128,256]{2,0,1:T(4,128)S(1)}, f32[4,128,256]{2,0,1:T(4,128)}, u32[]{:S(2)}) copy-start(f32[4,128,256]{2,0,1:T(4,128)} %custom-call.9) | copy-start | bytes 1572868
  105.6 67.8 %reduce-scatter.5.cloned.1.call-start = ((), (), s32[]{:S(2)}) async-start(), calls=%async_computation.9 | async-start | bytes 98304 | tf_op jit(solution)/shard_map/reduce_scatter | solution.py:109
Sparse Core Ops, SparseCore 0:
  105.7 55.8 reduce-scatter.2
  164.5 8.8 reduce-scatter.4
where the time goes:
time: 181 us; the launch traced here: 180 us
  waiting for transfers between devices  85.9 us (47%)
  blocking collectives  26.5 us (15%)
  local copies, waits for them, and re-layouts  19.3 us (11%)
  between operations  14.3 us (8%)
  matrix products  11.8 us (7%)
  other arithmetic  11.6 us (6%)
  starting transfers between devices  10.6 us (6%)
    reduce_scatter x1, waiting for transfers between devices, shards(): lax.psum_scatter(local_gradient, 'dev', scatter_dimension=0, tiled=True)  55.9 us
    all_to_all x1, blocking collectives, shards(): lax.all_to_all(lax.all_to_all(wanted.reshape(groups, owners, capacity), '...  12.2 us
    reduce_scatter x1, waiting for transfers between devices, shards(): lax.psum_scatter(partial_sum, 'grp', scatter_dimension=1, tiled=True)  11.7 us
    dot_general x4, matrix products, table_one(): jnp.einsum('cmk,c->mk', code_onehot(code_one), weight_one, precision=lax....  8.72 us
    all_to_all x1, blocking collectives, shards(): lax.all_to_all(wanted.reshape(groups, owners, capacity), 'grp', split_axi...  7.82 us
    all_to_all x1, waiting for transfers between devices, shards(): lax.all_to_all(lax.all_to_all(found_rows, 'grp', split_axis=0, concat_axi...  7.51 us
    dynamic_update_slice x4, local copies, waits for them, and re-layouts, fetched_terms(): weight_table = lax.map(table_one, (code_rows, weight))  7.34 us
    all_to_all x1, blocking collectives, shards(): lax.all_to_all(found_codes, 'grp', split_axis=0, concat_axis=0, tiled=True)  6.5 us
  transfers between devices with their start and end apart: 5, of which 5 were waited for; matrix products, arithmetic and copies ran while one was open for 6% of the time, Pallas kernels for 0%

commit v1 on v0

--- a/solution.py
+++ b/solution.py
@@ -1,6 +1,10 @@
+import functools
+
 import jax
 import jax.numpy as jnp
 from jax import lax
+from jax.experimental import pallas as pl
+from jax.experimental.pallas import tpu as pltpu
 from jax.sharding import PartitionSpec as P
 
 D = 1024
@@ -8,6 +12,256 @@
 K = 256
 C = 32
 SUB = 8
+
+LANE = 128
+TILES = D // LANE
+SPT = LANE // SUB
+QN = 4
+HALF = TILES // 2
+ROWS = HALF * QN + SPT + 1
+HIGHEST = lax.Precision.HIGHEST
+
+
+def iota(shape, axis):
+    return lax.broadcasted_iota(jnp.int32, shape, axis)
+
+
+def place():
+    return lax.axis_index("grp"), lax.axis_index("dev")
+
+
+def pack_kernel(q_ref, codes_ref, owner_ref, local_ref, out_ref, codes_t):
+    codes_t[...] = codes_ref[...].astype(jnp.float32).T
+    owner, local = owner_ref[...], local_ref[...]
+    diagonal = iota((C, C), 0) == iota((C, C), 1)
+    row = jnp.zeros((1, LANE), jnp.float32)
+    for q in range(QN):
+        owner_col = jnp.sum(jnp.where(diagonal, owner[q : q + 1, :], 0), axis=1, keepdims=True)
+        local_col = jnp.sum(jnp.where(diagonal, local[q : q + 1, :], 0), axis=1, keepdims=True)
+        hit = owner_col + q * C == iota((C, LANE), 1)
+        row += jnp.sum(
+            jnp.where(hit, local_col.astype(jnp.float32), 0.0), axis=0, keepdims=True
+        )
+    for p in range(C):
+        tile, core = (p // 16) * 4 + p % 4, p % 2
+        base = p * ROWS
+        for i in range(HALF):
+            t = 2 * i + core
+            out_ref[base + i * QN : base + (i + 1) * QN, :] = q_ref[:, t * LANE : (t + 1) * LANE]
+        first = base + HALF * QN
+        out_ref[first : first + SPT, :] = codes_t[tile * SPT : (tile + 1) * SPT, :]
+        out_ref[first + SPT : first + SPT + 1, :] = row
+
+
+def recon_kernel(codes_ref, other_ref, book_ref, out_ref, book_t, codes_t):
+    core = lax.rem(lax.axis_index("dev"), 2)
+    for block, ref in enumerate((codes_ref, other_ref)):
+        codes_t[block * M : (block + 1) * M, :] = ref[...].T
+    for i in range(HALF):
+        t = 2 * i + core
+        book = book_ref[:, pl.ds(pl.multiple_of(t * LANE, LANE), LANE)]
+        book_t[0] = book[:LANE, :].T
+        book_t[1] = book[LANE:, :].T
+        for block in range(2):
+            first = pl.multiple_of(block * M + t * SPT, SPT)
+            rows = codes_t[pl.ds(first, SPT), :]
+            for m in range(SPT):
+                code = jnp.broadcast_to(rows[m : m + 1, :], (SUB, LANE))
+                index = lax.bitwise_and(code, LANE - 1)
+                low = jnp.take_along_axis(book_t[0, m * SUB : (m + 1) * SUB, :], index, axis=1)
+                high = jnp.take_along_axis(book_t[1, m * SUB : (m + 1) * SUB, :], index, axis=1)
+                out_ref[i, block, m * SUB : (m + 1) * SUB, :] = jnp.where(code >= LANE, high, low)
+
+
+def query_rows(got_ref, row):
+    return jnp.concatenate([got_ref[pl.ds(row + q, C, stride=ROWS), :] for q in range(QN)], axis=0)
+
+
+def score_kernel(got_ref, docs_ref, other_ref, recon_ref, out_ref):
+    group, dev = place()
+    me = group * 16 + dev
+    core = lax.rem(dev, 2)
+    exact = [jnp.zeros((LANE, LANE), jnp.float32)] * 2
+    student = [jnp.zeros((LANE, LANE), jnp.float32)] * 2
+    for i in range(HALF):
+        columns = pl.ds(pl.multiple_of((2 * i + core) * LANE, LANE), LANE)
+        query = query_rows(got_ref, i * QN)
+        for block, ref in enumerate((docs_ref, other_ref)):
+            exact[block] += lax.dot_general(
+                query, ref[:, columns], (((1,), (1,)), ((), ())),
+                precision=HIGHEST, preferred_element_type=jnp.float32,
+            )
+            student[block] += jnp.dot(
+                query, recon_ref[i, block], precision=HIGHEST, preferred_element_type=jnp.float32
+            )
+    asked = got_ref[pl.ds(ROWS - 1, C, stride=ROWS), :]
+    lanes = iota((C, LANE), 1)
+    wide = iota((LANE, LANE), 1)
+    diagonal = iota((LANE, LANE), 0) == wide
+    rows = []
+    for block in range(2):
+        owner = me if block == 0 else me + 1 - 2 * core
+        local = jnp.concatenate(
+            [
+                jnp.sum(jnp.where(lanes == q * C + owner, asked, 0.0), axis=1, keepdims=True)
+                for q in range(QN)
+            ],
+            axis=0,
+        ).astype(jnp.int32)
+        hit = wide == local
+        for scores in (exact[block], student[block]):
+            column = jnp.sum(jnp.where(hit, scores, 0.0), axis=1, keepdims=True)
+            rows.append(jnp.sum(jnp.where(diagonal, column, 0.0), axis=0, keepdims=True))
+    mine = jnp.concatenate(rows, axis=0)
+    for p in range(C):
+        out_ref[p] = mine
+
+
+def pair_kernel(got_ref, out_ref):
+    asked = got_ref[pl.ds(ROWS - 1, C, stride=ROWS), :]
+    asked = jnp.concatenate([asked, jnp.zeros((LANE - C, LANE), jnp.float32)], axis=0).T
+    local = jnp.concatenate([asked[q * C : (q + 1) * C, :C] for q in range(QN)], axis=1)
+    local = local.astype(jnp.int32)
+    for o in range(C):
+        index = jnp.broadcast_to(local[o : o + 1, :], (SUB, LANE))
+        for half in range(2):
+            first = o * ROWS + HALF * QN + half * SUB
+            codes = got_ref[first : first + SUB, :]
+            out_ref[o, half * SUB : (half + 1) * SUB, :] = jnp.take_along_axis(codes, index, axis=1)
+
+
+def log_parts(scores):
+    top = jnp.max(scores, axis=0, keepdims=True)
+    shifted = scores - top
+    powers = jnp.exp(shifted)
+    total = jnp.sum(powers, axis=0, keepdims=True)
+    return powers / total, shifted - jnp.log(total)
+
+
+def gradient_kernel(scores_ref, pairs_ref, got_ref, *refs):
+    own_ref, core_ref, x_ref, both_ref, loss_ref, weight, table = refs
+    group, dev = place()
+    me = group * 16 + dev
+    low = lax.rem(dev, 4)
+    odd = lax.rem(iota((C, LANE), 0), 2) == 1
+
+    def joined(mine, other):
+        swapped = jnp.where(odd, pltpu.roll(other, 1, 0), pltpu.roll(other, C - 1, 0))
+        return mine + swapped
+
+    exact = joined(scores_ref[:, 0, :], scores_ref[:, 2, :])
+    student = joined(scores_ref[:, 1, :], scores_ref[:, 3, :])
+    teacher, log_teacher = log_parts(exact)
+    soft, log_soft = log_parts(student)
+    loss = jnp.sum(teacher * (log_teacher - log_soft), axis=0, keepdims=True)
+    lanes = iota((1, LANE), 1)
+    for q in range(QN):
+        loss_ref[q] = jnp.sum(jnp.where(lanes == q * C + me, loss, 0.0))
+    weight[...] = soft - teacher
+    span = 4 * 16
+    first = lax.div(dev, 4) * span
+    words = [(iota((SUB, LANE), 0) + (first + v * SUB)).astype(jnp.float32) for v in range(span // SUB)]
+
+    @pl.loop(0, SPT)
+    def _(m):
+        total = [jnp.zeros((SUB, LANE), jnp.float32)] * len(words)
+        for o in range(C):
+            code = jnp.broadcast_to(pairs_ref[o, pl.ds(m, 1), :], (SUB, LANE))
+            share = jnp.broadcast_to(weight[o : o + 1, :], (SUB, LANE))
+            for v, word in enumerate(words):
+                total[v] += jnp.where(code == word, share, 0.0)
+        for v in range(len(words)):
+            table[pl.ds(pl.multiple_of(m * span + v * SUB, SUB), SUB), :] = total[v]
+
+    row = (group * 2 + lax.div(low, 2)) * QN
+    query = query_rows(got_ref, row)
+    subspace = lax.div(iota((span, LANE), 1), SUB)
+    result = jnp.zeros((span, LANE), jnp.float32)
+    for m in range(SPT):
+        product = jnp.dot(
+            table[m * span : (m + 1) * span, :], query,
+            precision=HIGHEST, preferred_element_type=jnp.float32,
+        )
+        result += jnp.where(subspace == m, product, 0.0)
+    for i in range(4):
+        block = result[i * 16 : (i + 1) * 16, :]
+        for ref, who in ((own_ref, 0), (core_ref, 1), (x_ref, 2), (both_ref, 3)):
+            @pl.when(low == (i ^ who))
+            def _(ref=ref, block=block):
+                ref[...] = block
+
+
+def vmem(n):
+    return [pl.BlockSpec(memory_space=pltpu.VMEM)] * n
+
+
+def call(kernel, outs, n_in, scratch=(), out_specs=None, flops=0, moved=0):
+    return pl.pallas_call(
+        kernel,
+        out_shape=outs,
+        in_specs=vmem(n_in),
+        out_specs=out_specs,
+        scratch_shapes=list(scratch),
+        compiler_params=pltpu.CompilerParams(vmem_limit_bytes=40 * 1024 * 1024),
+        cost_estimate=pl.CostEstimate(flops=flops, bytes_accessed=moved, transcendentals=0),
+    )
+
+
+def f32(*shape):
+    return jax.ShapeDtypeStruct(shape, jnp.float32)
+
+
+def by_xor(value, bits, count):
+    return lax.ppermute(value, "dev", [(i, i ^ bits) for i in range(count)])
+
+
+def shards_once(queries, documents, doc_codes, codebook, candidate_owner, candidate_local):
+    owners = lax.axis_size("dev")
+    everyone = ("grp", "dev")
+    other_docs = by_xor(documents, 1, owners)
+    other_codes = by_xor(doc_codes, 1, owners)
+    sent = call(
+        pack_kernel, f32(C * ROWS, LANE), 4, [pltpu.VMEM((M, LANE), jnp.float32)], vmem(1)[0], 0, 1 << 20
+    )(queries, doc_codes, candidate_owner, candidate_local)
+    got = lax.all_to_all(
+        sent.reshape(C, ROWS, 1, LANE), everyone, split_axis=0, concat_axis=0, tiled=True
+    ).reshape(C * ROWS, LANE)
+    recon = call(
+        recon_kernel,
+        f32(HALF, 2, LANE, LANE),
+        3,
+        [pltpu.VMEM((2, LANE, LANE), jnp.float32), pltpu.VMEM((2 * M, LANE), jnp.int32)],
+        vmem(1)[0],
+        1 << 22,
+        1 << 21,
+    )(doc_codes, other_codes, codebook)
+    scores = call(score_kernel, f32(C, 4, LANE), 4, (), vmem(1)[0], 1 << 27, 1 << 21)(
+        got, documents, other_docs, recon
+    )
+    all_scores = lax.all_to_all(scores, everyone, split_axis=0, concat_axis=0, tiled=True)
+    pairs = call(pair_kernel, f32(C, SPT, LANE), 1, (), vmem(1)[0], 1 << 20, 1 << 20)(got)
+    own, core, across, both, query_loss = call(
+        gradient_kernel,
+        (f32(16, LANE),) * 4 + (f32(QN),),
+        3,
+        [pltpu.VMEM((C, LANE), jnp.float32), pltpu.VMEM((SPT * 64, LANE), jnp.float32)],
+        tuple(vmem(4)) + (pl.BlockSpec(memory_space=pltpu.SMEM),),
+        1 << 28,
+        1 << 21,
+    )(all_scores, pairs, got)
+    near = by_xor(jnp.stack([core, both]), 1, owners)
+    far = by_xor(jnp.stack([across, near[1]]), 2, owners)
+    dev = lax.axis_index("dev")
+    odd_core, odd_x = lax.rem(dev, 2) == 1, lax.rem(lax.div(dev, 2), 2) == 1
+
+    def pair(mine, other):
+        return jnp.where(odd_core, jnp.concatenate([other, mine], 1), jnp.concatenate([mine, other], 1))
+
+    here, there = pair(own, near[0]), pair(far[0], far[1])
+    gradient = jnp.where(
+        odd_x, jnp.concatenate([there, here], 1), jnp.concatenate([here, there], 1)
+    )
+    return gradient, query_loss
 
 
 def slot_positions(candidate_owner, capacity):
@@ -64,7 +318,7 @@
     return (query_loss, gradient.reshape(K, D))
 
 
-def shards(queries, documents, doc_codes, codebook, candidate_owner, candidate_local):
+def shards_any(queries, documents, doc_codes, codebook, candidate_owner, candidate_local):
     groups = lax.axis_size("grp")
     owners = lax.axis_size("dev")
     query_count = queries.shape[0]
@@ -120,4 +374,10 @@
         P(("grp", "dev"), None),
     )
     out_specs = (P("dev", "grp"), P(("grp", "dev")))
+
+    def shards(queries, documents, *rest):
+        once = dict(mesh.shape) == {"grp": 2, "dev": 16}
+        once = once and queries.shape == (QN, D) and documents.shape == (LANE, D)
+        return (shards_once if once else shards_any)(queries, documents, *rest)
+
     return jax.shard_map(shards, mesh=mesh, in_specs=in_specs, out_specs=out_specs, check_vma=False)

time: 181 us -> 49.9 us (0.28)
  waiting for transfers between devices: 85.9 us -> 26.1 us
  blocking collectives: 26.5 us -> 0 us
  local copies, waits for them, and re-layouts: 19.3 us -> 2.93 us
  between operations: 14.3 us -> 0.71 us
  matrix products: 11.8 us -> 0 us
  other arithmetic: 11.6 us -> 0.64 us
  Pallas kernels: 0 us -> 8 us
    reduce_scatter x2 -> x0, waiting for transfers between devices: 67.7 us -> none  [the longest x1 55.9 us: shards(): lax.psum_scatter(local_gradient, 'dev', scatter_dimension=0, tiled=True)]
    all_to_all x3 -> x0, blocking collectives: 26.5 us -> none  [the longest x1 12.2 us: shards(): lax.all_to_all(lax.all_to_all(wanted.reshape(groups, owners, capacity), '...]
    dot_general x7 -> x0, matrix products: 11.8 us -> none  [the longest x4 8.72 us: table_one(): jnp.einsum('cmk,c->mk', code_onehot(code_one), weight_one, precision=lax....]
    pallas_call x0 -> x5, Pallas kernels: none -> 8 us  [the longest x1 3.59 us: shards_once(): call(gradient_kernel, (f32(16, LANE),) * 4 + (f32(QN),), 3, [pltpu.VMEM((...]
    dynamic_update_slice x8 -> x0, local copies, waits for them, and re-layouts: 7.47 us -> none  [the longest x4 7.34 us: fetched_terms(): weight_table = lax.map(table_one, (code_rows, weight))]
    dot_general x4 -> x0, other arithmetic: 5.94 us -> none  [student_one(): jnp.einsum('cmk,mk->c', code_onehot(code_one), lookup_one, precision=lax....]
    ppermute x0 -> x4, waiting for transfers between devices: none -> 5.82 us  [by_xor(): return lax.ppermute(value, 'dev', [(i, i ^ bits) for i in range(count)])]
    gather x4 -> x0, local copies, waits for them, and re-layouts: 3.74 us -> none  [the longest x1 1.49 us: shards(): doc_codes[doc_index].astype(jnp.float32)]
  transfers between devices with their start and end apart: 5 -> 6, of which waited for: 5 -> 5; matrix products, arithmetic and copies ran while one was open for 6% -> 0% of each run, Pallas kernels for 0% -> 3%
where the time goes in v1:
time: 49.9 us; the launch traced here: 49.5 us
  waiting for transfers between devices  26.1 us (52%)
  starting transfers between devices  11.1 us (22%)
  Pallas kernels  8 us (16%)
  local copies, waits for them, and re-layouts  2.93 us (6%)
  between operations  0.71 us (1%)
  other arithmetic  0.64 us (1%)
    all_to_all x1, waiting for transfers between devices, shards_once(): lax.all_to_all(sent.reshape(C, ROWS, 1, LANE), everyone, split_axis=0, co...  13.3 us
    all_to_all x1, starting transfers between devices, shards_once(): lax.all_to_all(sent.reshape(C, ROWS, 1, LANE), everyone, split_axis=0, co...  7.3 us
    all_to_all x1, waiting for transfers between devices, shards_once(): lax.all_to_all(scores, everyone, split_axis=0, concat_axis=0, tiled=True)  7.02 us
    ppermute x4, waiting for transfers between devices, by_xor(): return lax.ppermute(value, 'dev', [(i, i ^ bits) for i in range(count)])  5.82 us
    pallas_call x1, Pallas kernels, shards_once(): call(gradient_kernel, (f32(16, LANE),) * 4 + (f32(QN),), 3, [pltpu.VMEM((...  3.59 us
    unnamed x14, local copies, waits for them, and re-layouts  2.92 us
    all_to_all x1, starting transfers between devices, shards_once(): lax.all_to_all(scores, everyone, split_axis=0, concat_axis=0, tiled=True)  2.57 us
    pallas_call x1, Pallas kernels, shards_once(): call(score_kernel, f32(C, 4, LANE), 4, (), vmem(1)[0], 1 << 27, 1 << 21)  2.16 us
  transfers between devices with their start and end apart: 6, of which 5 were waited for; matrix products, arithmetic and copies ran while one was open for 0% of the time, Pallas kernels for 3%

profile of v1, /device:TPU:0, one launch (start us, length us, event | category | flops | bytes accessed | tf_op | source)
XLA Modules:
  0.0 49.5 jit_solution(7791939002196705564)
XLA Ops:
  0.6 0.0 copy-start.2
  0.6 0.8 %copy-done.2 = s32[128,128]{1,0:T(8,128)S(1)} copy-done((s32[128,128]{1,0:T(8,128)S(1)}, s32[128,128]{1,0:T(8,128)}, u32[]{:S(2)}) %copy-start.2) | copy-done | bytes 65560
  1.5 0.0 copy-start.4
  1.5 0.7 %copy-done.4 = f32[4,1024]{1,0:T(4,128)S(1)} copy-done((f32[4,1024]{1,0:T(4,128)S(1)}, f32[4,1024]{1,0:T(4,128)}, u32[]{:S(2)}) %copy-start.4) | copy-done | bytes 16408
  2.2 0.0 copy-start.5
  2.2 0.7 %copy-done.5 = s32[4,32]{1,0:T(4,128)S(1)} copy-done((s32[4,32]{1,0:T(4,128)S(1)}, s32[4,32]{1,0:T(4,128)}, u32[]{:S(2)}) %copy-start.5) | copy-done | bytes 536
  2.9 0.0 copy-start.6
  2.9 0.7 %copy-done.6 = s32[4,32]{1,0:T(4,128)S(1)} copy-done((s32[4,32]{1,0:T(4,128)S(1)}, s32[4,32]{1,0:T(4,128)}, u32[]{:S(2)}) %copy-start.6) | copy-done | bytes 536
  3.6 0.0 copy-start
  3.6 1.0 %shard_map.77 = f32[1056,128]{1,0:T(8,128)} custom-call(f32[4,1024]{1,0:T(4,128)S(1)} %copy-done.4, s32[128,128]{1,0:T(8,128)S(1)} %copy-done.2, s32[4,32]{1,0:T(4,128)S(1)} %copy-done.5, s32[4,32]{1,0:T(4,128)S(1)} %copy-done.6), custom_call_target="tpu_custom_call" | custom-call | bytes 1048576 | tf_op jit(solution)/shard_map/pallas_call | solution.py:223
  4.6 0.0 copy-start.1
  4.6 0.0 copy-start.3
  4.6 7.3 %all-to-all-start = ((f32[32,33,1,128]{3,2,1,0:T(1,128)}), f32[32,33,1,128]{3,2,1,0:T(1,128)S(1)}, u32[]{:S(2)}, u32[]{:S(2)}) async-start(f32[32,33,1,128]{3,2,1,0:T(1,128)} %bitcast), calls=%async_computation | async-start | bytes 1081344 | tf_op jit(solution)/shard_map/all_to_all | solution.py:226
  11.9 0.0 copy-done.1
  11.9 0.3 collective-permute-start
  12.2 0.0 copy-done.3
  12.2 0.3 collective-permute-start.1
  12.5 1.5 %collective-permute-done.1.other_ref = s32[128,128]{1,0:T(8,128)S(1)} collective-permute-done((s32[128,128]{1,0:T(8,128)S(1)}, s32[128,128]{1,0:T(8,128)S(1)}, u32[]{:S(2)}, u32[]{:S(2)}) %collective-permute-start.1) | collective-permute-done | bytes 65568 | tf_op jit(solution)/shard_map/ppermute | solution.py:215
  13.9 0.0 copy-done
  14.0 0.9 %shard_map.78.recon_ref = f32[4,2,128,128]{3,2,1,0:T(8,128)S(1)} custom-call(s32[128,128]{1,0:T(8,128)S(1)} %copy-done.3, s32[128,128]{1,0:T(8,128)S(1)} %collective-permute-done.1.other_ref, f32[256,1024]{1,0:T(8,128)S(1)} %copy-done), custom_call_target="tpu_custom_call" | custom-call | flops 4194304 | bytes 2097152 | tf_op jit(solution)/shard_map/pallas_call | solution.py:229
  14.8 0.0 collective-permute-done.other_ref
  14.8 13.3 %all-to-all-done = f32[32,33,1,128]{3,2,1,0:T(1,128)S(1)} async-done(((f32[32,33,1,128]{3,2,1,0:T(1,128)}), f32[32,33,1,128]{3,2,1,0:T(1,128)S(1)}, u32[]{:S(2)}, u32[]{:S(2)}) %all-to-all-start) | async-done | bytes 540704 | tf_op jit(solution)/shard_map/all_to_all | solution.py:226
  28.1 2.2 %shard_map.79 = f32[32,4,128]{2,1,0:T(4,128)} custom-call(f32[1056,128]{1,0:T(8,128)S(1)} %bitcast.11, f32[128,1024]{1,0:T(8,128)S(1)} %copy-done.1, f32[128,1024]{1,0:T(8,128)S(1)} %collective-permute-done.other_ref, f32[4,2,128,128]{3,2,1,0:T(8,128)S(1)} %shard_map.78.recon_ref), custom_call_target="tpu_custom_call" | custom-call | flops 134217728 | bytes 2097152 | tf_op jit(solution)/shard_map/pallas_call | solution.py:238
  30.3 2.6 %all-to-all-start.1 = ((f32[32,4,128]{2,1,0:T(4,128)}), f32[32,4,128]{2,1,0:T(4,128)S(1)}, u32[]{:S(2)}, u32[]{:S(2)}) async-start(f32[32,4,128]{2,1,0:T(4,128)} %shard_map.79), calls=%async_computation.1 | async-start | bytes 131072 | tf_op jit(solution)/shard_map/all_to_all | solution.py:241
  32.9 0.4 shard_map.80.pairs_ref
  33.3 7.0 %all-to-all-done.1.scores_ref = f32[32,4,128]{2,1,0:T(4,128)S(1)} async-done(((f32[32,4,128]{2,1,0:T(4,128)}), f32[32,4,128]{2,1,0:T(4,128)S(1)}, u32[]{:S(2)}, u32[]{:S(2)}) %all-to-all-start.1) | async-done | bytes 65568 | tf_op jit(solution)/shard_map/all_to_all | solution.py:241
  40.3 3.6 %shard_map.81 = (f32[16,128]{1,0:T(8,128)S(1)}, f32[16,128]{1,0:T(8,128)S(1)}, f32[16,128]{1,0:T(8,128)S(1)}, f32[16,128]{1,0:T(8,128)S(1)}, f32[4]{0:T(128)}) custom-call(f32[32,4,128]{2,1,0:T(4,128)S(1)} %all-to-all-done.1.scores_ref, f32[32,16,128]{2,1,0:T(8,128)S(1)} %shard_map.80.pairs_ref, f32[1056,128]{1,0:T(8,128)S(1)} %bitcast.13), custom_call_target="tpu_custom_call" | custom-call | flops 268435456 | bytes 2097152 | tf_op jit(solution)/shard_map/pallas_call | solution.py:243
  43.9 0.2 collective-permute-start.2
  44.1 1.1 %collective-permute-done.2 = f32[2,16,128]{2,1,0:T(8,128)S(1)} collective-permute-done((f32[2,16,128]{2,1,0:T(8,128)S(1)}, f32[2,16,128]{2,1,0:T(8,128)S(1)}, u32[]{:S(2)}, u32[]{:S(2)}) %collective-permute-start.2) | collective-permute-done | bytes 16416 | tf_op jit(solution)/shard_map/ppermute | solution.py:215
  45.2 0.5 collective-permute-start.3
  45.6 3.3 %collective-permute-done.3 = f32[2,16,128]{2,1,0:T(8,128)S(1)} collective-permute-done((f32[2,16,128]{2,1,0:T(8,128)S(1)}, f32[2,16,128]{2,1,0:T(8,128)S(1)}, u32[]{:S(2)}, u32[]{:S(2)}) %collective-permute-start.3) | collective-permute-done | bytes 16416 | tf_op jit(solution)/shard_map/ppermute | solution.py:215
  48.9 0.6 %maximum_select_fusion = f32[16,512]{1,0:T(8,128)} fusion(f32[16,256]{1,0:T(8,128)S(1)} %maximum_select_fusion.2, f32[16,256]{1,0:T(8,128)S(1)} %maximum_select_fusion.1, pred[]{:T(512)S(6)} %eq.6), kind=kLoop, calls=%fused_computation | loop fusion | flops 24576 | bytes 65537 | tf_op jit(solution)/shard_map/jit(_where)/select_n | solution.py:261
  (6 shorter events, 0.0 us)
Async XLA Ops:
  0.6 0.8 %copy-start.2 = (s32[128,128]{1,0:T(8,128)S(1)}, s32[128,128]{1,0:T(8,128)}, u32[]{:S(2)}) copy-start(s32[128,128]{1,0:T(8,128)} %codes_ref.3) | copy-start | bytes 196612
  1.5 0.7 %copy-start.4 = (f32[4,1024]{1,0:T(4,128)S(1)}, f32[4,1024]{1,0:T(4,128)}, u32[]{:S(2)}) copy-start(f32[4,1024]{1,0:T(4,128)} %q_ref.1) | copy-start | bytes 49156
  2.2 0.7 %copy-start.5 = (s32[4,32]{1,0:T(4,128)S(1)}, s32[4,32]{1,0:T(4,128)}, u32[]{:S(2)}) copy-start(s32[4,32]{1,0:T(4,128)} %owner_ref.1) | copy-start | bytes 1540
  2.9 0.7 %copy-start.6 = (s32[4,32]{1,0:T(4,128)S(1)}, s32[4,32]{1,0:T(4,128)}, u32[]{:S(2)}) copy-start(s32[4,32]{1,0:T(4,128)} %local_ref.1) | copy-start | bytes 1540
  3.6 10.4 %copy-start = (f32[256,1024]{1,0:T(8,128)S(1)}, f32[256,1024]{1,0:T(8,128)}, u32[]{:S(2)}) copy-start(f32[256,1024]{1,0:T(8,128)} %book_ref.1) | copy-start | bytes 3145732
  4.6 7.3 %copy-start.1 = (f32[128,1024]{1,0:T(8,128)S(1)}, f32[128,1024]{1,0:T(8,128)}, u32[]{:S(2)}) copy-start(f32[128,1024]{1,0:T(8,128)} %docs_ref.1) | copy-start | bytes 1572868
  4.6 7.6 %copy-start.3 = (s32[128,128]{1,0:T(8,128)S(1)}, s32[128,128]{1,0:T(8,128)}, u32[]{:S(2)}) copy-start(s32[128,128]{1,0:T(8,128)} %codes_ref.3) | copy-start | bytes 196612
  4.6 23.6 %all-to-all-start = ((f32[32,33,1,128]{3,2,1,0:T(1,128)}), f32[32,33,1,128]{3,2,1,0:T(1,128)S(1)}, u32[]{:S(2)}, u32[]{:S(2)}) async-start(f32[32,33,1,128]{3,2,1,0:T(1,128)} %bitcast), calls=%async_computation | async-start | bytes 1081344 | tf_op jit(solution)/shard_map/all_to_all | solution.py:226
  11.9 2.9 %collective-permute-start = (f32[128,1024]{1,0:T(8,128)S(1)}, f32[128,1024]{1,0:T(8,128)S(1)}, u32[]{:S(2)}, u32[]{:S(2)}) collective-permute-start(f32[128,1024]{1,0:T(8,128)S(1)} %copy-done.1), channel_id=1, source_target_pairs={{0,1},{1,0},{2,3},{3,2},{4,5},{5,4},{6,7},{7,6},{8,9},{9,8},{10,11... | collective-permute-start | bytes 1572872 | tf_op jit(solution)/shard_map/ppermute | solution.py:215
  12.2 1.8 %collective-permute-start.1 = (s32[128,128]{1,0:T(8,128)S(1)}, s32[128,128]{1,0:T(8,128)S(1)}, u32[]{:S(2)}, u32[]{:S(2)}) collective-permute-start(s32[128,128]{1,0:T(8,128)S(1)} %copy-done.3), channel_id=1, source_target_pairs={{0,1},{1,0},{2,3},{3,2},{4,5},{5,4},{6,7},{7,6},{8,9},{9,8},{10,11... | collective-permute-start | bytes 196616 | tf_op jit(solution)/shard_map/ppermute | solution.py:215
  30.3 10.0 %all-to-all-start.1 = ((f32[32,4,128]{2,1,0:T(4,128)}), f32[32,4,128]{2,1,0:T(4,128)S(1)}, u32[]{:S(2)}, u32[]{:S(2)}) async-start(f32[32,4,128]{2,1,0:T(4,128)} %shard_map.79), calls=%async_computation.1 | async-start | bytes 131072 | tf_op jit(solution)/shard_map/all_to_all | solution.py:241
  43.9 1.2 %collective-permute-start.2 = (f32[2,16,128]{2,1,0:T(8,128)S(1)}, f32[2,16,128]{2,1,0:T(8,128)S(1)}, u32[]{:S(2)}, u32[]{:S(2)}) collective-permute-start(f32[2,16,128]{2,1,0:T(8,128)S(1)} %pad_maximum_fusion), channel_id=1, source_target_pairs={{0,1},{1,0},{2,3},{3,2},{4,5},{5,4},{6,7},{7,6},{8,9},{9,8},{10,11... | collective-permute-start | bytes 49160 | tf_op jit(solution)/shard_map/ppermute | solution.py:215
  45.2 3.7 %collective-permute-start.3 = (f32[2,16,128]{2,1,0:T(8,128)S(1)}, f32[2,16,128]{2,1,0:T(8,128)S(1)}, u32[]{:S(2)}, u32[]{:S(2)}) collective-permute-start(f32[2,16,128]{2,1,0:T(8,128)S(1)} %pad_maximum_fusion.1), channel_id=1, source_target_pairs={{0,2},{1,3},{2,0},{3,1},{4,6},{5,7},{6,4},{7,5},{8,10},{9,11},{10,... | collective-permute-start | bytes 49160 | tf_op jit(solution)/shard_map/ppermute | solution.py:215

commit v2 on v1

--- a/solution.py
+++ b/solution.py
@@ -19,7 +19,6 @@
 QN = 4
 HALF = TILES // 2
 ROWS = HALF * QN + SPT + 1
-HIGHEST = lax.Precision.HIGHEST
 
 
 def iota(shape, axis):
@@ -30,7 +29,29 @@
     return lax.axis_index("grp"), lax.axis_index("dev")
 
 
-def pack_kernel(q_ref, codes_ref, owner_ref, local_ref, out_ref, codes_t):
+def fetch(pairs, sems):
+    copies = [pltpu.make_async_copy(src, dst, sems.at[i]) for i, (src, dst) in enumerate(pairs)]
+    for copy in copies:
+        copy.start()
+    for copy in copies:
+        copy.wait()
+
+
+def thirds(value):
+    first = value.astype(jnp.bfloat16)
+    rest = value - first.astype(jnp.float32)
+    second = rest.astype(jnp.bfloat16)
+    return first, second, (rest - second.astype(jnp.float32)).astype(jnp.bfloat16)
+
+
+def dot(a, b):
+    return jnp.dot(a, b, preferred_element_type=jnp.float32)
+
+
+def pack_kernel(*refs):
+    q_ref, codes_ref, owner_ref, local_ref = refs[5:9]
+    out_ref, codes_t, sems = refs[4], refs[9], refs[10]
+    fetch(list(zip(refs[:4], refs[5:9])), sems)
     codes_t[...] = codes_ref[...].astype(jnp.float32).T
     owner, local = owner_ref[...], local_ref[...]
     diagonal = iota((C, C), 0) == iota((C, C), 1)
@@ -53,47 +74,49 @@
         out_ref[first + SPT : first + SPT + 1, :] = row
 
 
-def recon_kernel(codes_ref, other_ref, book_ref, out_ref, book_t, codes_t):
+def owner_kernel(codes_ref, other_ref, book_ref, docs_ref, other_docs_ref, out_ref, book_t, codes_t):
     core = lax.rem(lax.axis_index("dev"), 2)
+
+    def put(i, column, value):
+        for level, part in enumerate(thirds(value)):
+            out_ref[level, i * LANE : (i + 1) * LANE, column * LANE : (column + 1) * LANE] = part
+
     for block, ref in enumerate((codes_ref, other_ref)):
         codes_t[block * M : (block + 1) * M, :] = ref[...].T
     for i in range(HALF):
         t = 2 * i + core
-        book = book_ref[:, pl.ds(pl.multiple_of(t * LANE, LANE), LANE)]
-        book_t[0] = book[:LANE, :].T
-        book_t[1] = book[LANE:, :].T
+        columns = pl.ds(pl.multiple_of(t * LANE, LANE), LANE)
+        for block, ref in enumerate((docs_ref, other_docs_ref)):
+            put(i, block, ref[:, columns].T)
+        book_t[0] = book_ref[:LANE, columns].T
+        book_t[1] = book_ref[LANE:, columns].T
         for block in range(2):
             first = pl.multiple_of(block * M + t * SPT, SPT)
             rows = codes_t[pl.ds(first, SPT), :]
+            made = []
             for m in range(SPT):
                 code = jnp.broadcast_to(rows[m : m + 1, :], (SUB, LANE))
                 index = lax.bitwise_and(code, LANE - 1)
                 low = jnp.take_along_axis(book_t[0, m * SUB : (m + 1) * SUB, :], index, axis=1)
                 high = jnp.take_along_axis(book_t[1, m * SUB : (m + 1) * SUB, :], index, axis=1)
-                out_ref[i, block, m * SUB : (m + 1) * SUB, :] = jnp.where(code >= LANE, high, low)
+                made.append(jnp.where(code >= LANE, high, low))
+            put(i, 2 + block, jnp.concatenate(made, axis=0))
 
 
 def query_rows(got_ref, row):
     return jnp.concatenate([got_ref[pl.ds(row + q, C, stride=ROWS), :] for q in range(QN)], axis=0)
 
 
-def score_kernel(got_ref, docs_ref, other_ref, recon_ref, out_ref):
+def score_kernel(got_ref, table_ref, out_ref):
     group, dev = place()
     me = group * 16 + dev
     core = lax.rem(dev, 2)
-    exact = [jnp.zeros((LANE, LANE), jnp.float32)] * 2
-    student = [jnp.zeros((LANE, LANE), jnp.float32)] * 2
-    for i in range(HALF):
-        columns = pl.ds(pl.multiple_of((2 * i + core) * LANE, LANE), LANE)
-        query = query_rows(got_ref, i * QN)
-        for block, ref in enumerate((docs_ref, other_ref)):
-            exact[block] += lax.dot_general(
-                query, ref[:, columns], (((1,), (1,)), ((), ())),
-                precision=HIGHEST, preferred_element_type=jnp.float32,
-            )
-            student[block] += jnp.dot(
-                query, recon_ref[i, block], precision=HIGHEST, preferred_element_type=jnp.float32
-            )
+    query = jnp.concatenate([query_rows(got_ref, i * QN) for i in range(HALF)], axis=1)
+    q0, q1, q2 = thirds(query)
+    t0, t1, t2 = table_ref[0], table_ref[1], table_ref[2]
+    scores = dot(q0, t2) + dot(q2, t0) + dot(q1, t1)
+    scores = scores + (dot(q0, t1) + dot(q1, t0))
+    scores = scores + dot(q0, t0)
     asked = got_ref[pl.ds(ROWS - 1, C, stride=ROWS), :]
     lanes = iota((C, LANE), 1)
     wide = iota((LANE, LANE), 1)
@@ -109,15 +132,24 @@
             axis=0,
         ).astype(jnp.int32)
         hit = wide == local
-        for scores in (exact[block], student[block]):
-            column = jnp.sum(jnp.where(hit, scores, 0.0), axis=1, keepdims=True)
+        for kind in range(2):
+            first = (kind * 2 + block) * LANE
+            column = jnp.sum(
+                jnp.where(hit, scores[:, first : first + LANE], 0.0), axis=1, keepdims=True
+            )
             rows.append(jnp.sum(jnp.where(diagonal, column, 0.0), axis=0, keepdims=True))
     mine = jnp.concatenate(rows, axis=0)
     for p in range(C):
         out_ref[p] = mine
 
 
-def pair_kernel(got_ref, out_ref):
+def pair_kernel(got_ref, out_ref, query_ref):
+    group, dev = place()
+    half = group * 2 + lax.div(lax.rem(dev, 4), 2)
+    first, second, _ = thirds(query_rows(got_ref, half * QN))
+    for rows in (slice(0, LANE), slice(LANE, 2 * LANE)):
+        query_ref[rows, :LANE] = first
+        query_ref[rows, LANE:] = second
     asked = got_ref[pl.ds(ROWS - 1, C, stride=ROWS), :]
     asked = jnp.concatenate([asked, jnp.zeros((LANE - C, LANE), jnp.float32)], axis=0).T
     local = jnp.concatenate([asked[q * C : (q + 1) * C, :C] for q in range(QN)], axis=1)
@@ -127,7 +159,8 @@
         for half in range(2):
             first = o * ROWS + HALF * QN + half * SUB
             codes = got_ref[first : first + SUB, :]
-            out_ref[o, half * SUB : (half + 1) * SUB, :] = jnp.take_along_axis(codes, index, axis=1)
+            found = jnp.take_along_axis(codes, index, axis=1)
+            out_ref[o, half * SUB : (half + 1) * SUB, :] = found
 
 
 def log_parts(scores):
@@ -138,7 +171,7 @@
     return powers / total, shifted - jnp.log(total)
 
 
-def gradient_kernel(scores_ref, pairs_ref, got_ref, *refs):
+def gradient_kernel(scores_ref, pairs_ref, query_ref, *refs):
     own_ref, core_ref, x_ref, both_ref, loss_ref, weight, table = refs
     group, dev = place()
     me = group * 16 + dev
@@ -157,7 +190,9 @@
     lanes = iota((1, LANE), 1)
     for q in range(QN):
         loss_ref[q] = jnp.sum(jnp.where(lanes == q * C + me, loss, 0.0))
-    weight[...] = soft - teacher
+    share = soft - teacher
+    for o in range(C):
+        weight[o] = jnp.broadcast_to(share[o : o + 1, :], (SUB, LANE))
     span = 4 * 16
     first = lax.div(dev, 4) * span
     words = [(iota((SUB, LANE), 0) + (first + v * SUB)).astype(jnp.float32) for v in range(span // SUB)]
@@ -167,22 +202,20 @@
         total = [jnp.zeros((SUB, LANE), jnp.float32)] * len(words)
         for o in range(C):
             code = jnp.broadcast_to(pairs_ref[o, pl.ds(m, 1), :], (SUB, LANE))
-            share = jnp.broadcast_to(weight[o : o + 1, :], (SUB, LANE))
+            part = weight[o]
             for v, word in enumerate(words):
-                total[v] += jnp.where(code == word, share, 0.0)
-        for v in range(len(words)):
-            table[pl.ds(pl.multiple_of(m * span + v * SUB, SUB), SUB), :] = total[v]
-
-    row = (group * 2 + lax.div(low, 2)) * QN
-    query = query_rows(got_ref, row)
+                total[v] += jnp.where(code == word, part, 0.0)
+        rows = pl.ds(pl.multiple_of(m * span, span), span)
+        first, second, _ = thirds(jnp.concatenate(total, axis=0))
+        table[rows, :LANE] = first
+        table[rows, LANE:] = second
+
     subspace = lax.div(iota((span, LANE), 1), SUB)
+    product = dot(table[...], query_ref[...])
+    product = product[:, :LANE] + product[:, LANE:]
     result = jnp.zeros((span, LANE), jnp.float32)
     for m in range(SPT):
-        product = jnp.dot(
-            table[m * span : (m + 1) * span, :], query,
-            precision=HIGHEST, preferred_element_type=jnp.float32,
-        )
-        result += jnp.where(subspace == m, product, 0.0)
+        result += jnp.where(subspace == m, product[m * span : (m + 1) * span, :], 0.0)
     for i in range(4):
         block = result[i * 16 : (i + 1) * 16, :]
         for ref, who in ((own_ref, 0), (core_ref, 1), (x_ref, 2), (both_ref, 3)):
@@ -195,14 +228,14 @@
     return [pl.BlockSpec(memory_space=pltpu.VMEM)] * n
 
 
-def call(kernel, outs, n_in, scratch=(), out_specs=None, flops=0, moved=0):
+def call(kernel, outs, n_in, scratch=(), out_specs=None, flops=0, moved=0, space=pltpu.VMEM, mib=8):
     return pl.pallas_call(
         kernel,
         out_shape=outs,
-        in_specs=vmem(n_in),
+        in_specs=[pl.BlockSpec(memory_space=space)] * n_in,
         out_specs=out_specs,
         scratch_shapes=list(scratch),
-        compiler_params=pltpu.CompilerParams(vmem_limit_bytes=40 * 1024 * 1024),
+        compiler_params=pltpu.CompilerParams(vmem_limit_bytes=mib * 1024 * 1024),
         cost_estimate=pl.CostEstimate(flops=flops, bytes_accessed=moved, transcendentals=0),
     )
 
@@ -221,34 +254,55 @@
     other_docs = by_xor(documents, 1, owners)
     other_codes = by_xor(doc_codes, 1, owners)
     sent = call(
-        pack_kernel, f32(C * ROWS, LANE), 4, [pltpu.VMEM((M, LANE), jnp.float32)], vmem(1)[0], 0, 1 << 20
+        pack_kernel,
+        f32(C * ROWS, LANE),
+        4,
+        [
+            pltpu.VMEM((QN, D), jnp.float32),
+            pltpu.VMEM((LANE, M), jnp.int32),
+            pltpu.VMEM((QN, C), jnp.int32),
+            pltpu.VMEM((QN, C), jnp.int32),
+            pltpu.VMEM((M, LANE), jnp.float32),
+            pltpu.SemaphoreType.DMA((4,)),
+        ],
+        vmem(1)[0],
+        0,
+        1 << 20,
+        pl.ANY,
+        62,
     )(queries, doc_codes, candidate_owner, candidate_local)
     got = lax.all_to_all(
         sent.reshape(C, ROWS, 1, LANE), everyone, split_axis=0, concat_axis=0, tiled=True
     ).reshape(C * ROWS, LANE)
-    recon = call(
-        recon_kernel,
-        f32(HALF, 2, LANE, LANE),
-        3,
+    table = call(
+        owner_kernel,
+        jax.ShapeDtypeStruct((3, HALF * LANE, 4 * LANE), jnp.bfloat16),
+        5,
         [pltpu.VMEM((2, LANE, LANE), jnp.float32), pltpu.VMEM((2 * M, LANE), jnp.int32)],
         vmem(1)[0],
         1 << 22,
         1 << 21,
-    )(doc_codes, other_codes, codebook)
-    scores = call(score_kernel, f32(C, 4, LANE), 4, (), vmem(1)[0], 1 << 27, 1 << 21)(
-        got, documents, other_docs, recon
-    )
+    )(doc_codes, other_codes, codebook, documents, other_docs)
+    scores = call(score_kernel, f32(C, 4, LANE), 2, (), vmem(1)[0], 1 << 27, 1 << 21)(got, table)
     all_scores = lax.all_to_all(scores, everyone, split_axis=0, concat_axis=0, tiled=True)
-    pairs = call(pair_kernel, f32(C, SPT, LANE), 1, (), vmem(1)[0], 1 << 20, 1 << 20)(got)
+    pairs, columns = call(
+        pair_kernel,
+        (f32(C, SPT, LANE), jax.ShapeDtypeStruct((2 * LANE, 2 * LANE), jnp.bfloat16)),
+        1,
+        (),
+        tuple(vmem(2)),
+        1 << 20,
+        1 << 20,
+    )(got)
     own, core, across, both, query_loss = call(
         gradient_kernel,
         (f32(16, LANE),) * 4 + (f32(QN),),
         3,
-        [pltpu.VMEM((C, LANE), jnp.float32), pltpu.VMEM((SPT * 64, LANE), jnp.float32)],
+        [pltpu.VMEM((C, SUB, LANE), jnp.float32), pltpu.VMEM((SPT * 64, 2 * LANE), jnp.bfloat16)],
         tuple(vmem(4)) + (pl.BlockSpec(memory_space=pltpu.SMEM),),
         1 << 28,
         1 << 21,
-    )(all_scores, pairs, got)
+    )(all_scores, pairs, columns)
     near = by_xor(jnp.stack([core, both]), 1, owners)
     far = by_xor(jnp.stack([across, near[1]]), 2, owners)
     dev = lax.axis_index("dev")

time: 49.9 us -> 46.6 us (0.934)
  local copies, waits for them, and re-layouts: 2.93 us -> 1.05 us
  waiting for transfers between devices: 26.1 us -> 25 us
    unnamed x14 -> x6, local copies, waits for them, and re-layouts: 2.92 us -> 1.05 us
    all_to_all x1, waiting for transfers between devices: 13.3 us -> 12 us  [shards_once(): lax.all_to_all(sent.reshape(C, ROWS, 1, LANE), everyone, split_axis=0, co...]
  transfers between devices with their start and end apart: 6 -> 6, of which waited for: 5 -> 6; matrix products, arithmetic and copies ran while one was open for 0% -> 0% of each run, Pallas kernels for 3% -> 3%
where the time goes in v2:
time: 46.6 us; the launch traced here: 46.3 us
  waiting for transfers between devices  25 us (54%)
  starting transfers between devices  11.1 us (24%)
  Pallas kernels  7.9 us (17%)
  local copies, waits for them, and re-layouts  1.05 us (2%)
  between operations  0.7 us (2%)
  other arithmetic  0.64 us (1%)
    all_to_all x1, waiting for transfers between devices, shards_once(): lax.all_to_all(sent.reshape(C, ROWS, 1, LANE), everyone, split_axis=0, co...  12 us
    all_to_all x1, starting transfers between devices, shards_once(): lax.all_to_all(sent.reshape(C, ROWS, 1, LANE), everyone, split_axis=0, co...  7.3 us
    all_to_all x1, waiting for transfers between devices, shards_once(): lax.all_to_all(scores, everyone, split_axis=0, concat_axis=0, tiled=True)  7.01 us
    ppermute x4, waiting for transfers between devices, by_xor(): return lax.ppermute(value, 'dev', [(i, i ^ bits) for i in range(count)])  5.95 us
    pallas_call x1, Pallas kernels, shards_once(): call(gradient_kernel, (f32(16, LANE),) * 4 + (f32(QN),), 3, [pltpu.VMEM((...  3.12 us
    all_to_all x1, starting transfers between devices, shards_once(): lax.all_to_all(scores, everyone, split_axis=0, concat_axis=0, tiled=True)  2.55 us
    pallas_call x1, Pallas kernels, shards_once(): call(pack_kernel, f32(C * ROWS, LANE), 4, [pltpu.VMEM((QN, D), jnp.float3...  1.97 us
    pallas_call x1, Pallas kernels, shards_once(): call(score_kernel, f32(C, 4, LANE), 2, (), vmem(1)[0], 1 << 27, 1 << 21)  1.39 us
  transfers between devices with their start and end apart: 6, of which 6 were waited for; matrix products, arithmetic and copies ran while one was open for 0% of the time, Pallas kernels for 3%

profile of v2, /device:TPU:0, one launch (start us, length us, event | category | flops | bytes accessed | tf_op | source)
XLA Modules:
  0.0 46.3 jit_solution(13759043805274358214)
XLA Ops:
  0.6 0.0 copy-start.2
  0.6 0.0 copy-start
  0.7 2.0 %shard_map.77 = f32[1056,128]{1,0:T(8,128)} custom-call(f32[4,1024]{1,0:T(4,128)} %refs_0_.1, s32[128,128]{1,0:T(8,128)} %codes_ref.1, s32[4,32]{1,0:T(4,128)} %refs_2_.1, s32[4,32]{1,0:T(4,128)} %refs_3_.1), custom_call_target="tpu_custom_call" | custom-call | bytes 1048576 | tf_op jit(solution)/shard_map/pallas_call | solution.py:256
  2.6 7.3 %all-to-all-start = ((f32[32,33,1,128]{3,2,1,0:T(1,128)}), f32[32,33,1,128]{3,2,1,0:T(1,128)S(1)}, u32[]{:S(2)}, u32[]{:S(2)}) async-start(f32[32,33,1,128]{3,2,1,0:T(1,128)} %bitcast.16), calls=%async_computation | async-start | bytes 1081344 | tf_op jit(solution)/shard_map/all_to_all | solution.py:274
  9.9 0.3 collective-permute-start.1
  10.3 0.0 copy-done.2
  10.3 0.3 collective-permute-start
  10.5 1.5 %collective-permute-done.other_ref = s32[128,128]{1,0:T(8,128)S(1)} collective-permute-done((s32[128,128]{1,0:T(8,128)S(1)}, s32[128,128]{1,0:T(8,128)S(1)}, u32[]{:S(2)}, u32[]{:S(2)}) %collective-permute-start) | collective-permute-done | bytes 65568 | tf_op jit(solution)/shard_map/ppermute | solution.py:248
  12.0 0.1 collective-permute-done.1.other_docs_ref
  12.1 0.0 copy-done
  12.1 0.0 copy-start.1
  12.1 1.0 %copy-done.1 = f32[128,1024]{1,0:T(8,128)S(1)} copy-done((f32[128,1024]{1,0:T(8,128)S(1)}, f32[128,1024]{1,0:T(8,128)}, u32[]{:S(2)}) %copy-start.1) | copy-done | bytes 524312
  13.2 1.0 %shard_map.78.table_ref = bf16[3,512,512]{2,1,0:T(8,128)(2,1)S(1)} custom-call(s32[128,128]{1,0:T(8,128)S(1)} %copy-done.2, s32[128,128]{1,0:T(8,128)S(1)} %collective-permute-done.other_ref, f32[256,1024]{1,0:T(8,128)S(1)} %copy-done, f32[128,1024]{1,0:T(8,128)S(1)} %copy-done.1, f32[128,1024]{1,0:T(8,128)S(1)} %collective-permute-done.1.other_docs_ref), custom_call_target="tpu_custom_call" | custom-call | flops 4194304 | bytes 2097152 | tf_op jit(solution)/shard_map/pallas_call | solution.py:277
  14.2 12.0 %all-to-all-done = f32[32,33,1,128]{3,2,1,0:T(1,128)S(1)} async-done(((f32[32,33,1,128]{3,2,1,0:T(1,128)}), f32[32,33,1,128]{3,2,1,0:T(1,128)S(1)}, u32[]{:S(2)}, u32[]{:S(2)}) %all-to-all-start) | async-done | bytes 540704 | tf_op jit(solution)/shard_map/all_to_all | solution.py:274
  26.2 1.4 %shard_map.79 = f32[32,4,128]{2,1,0:T(4,128)} custom-call(f32[1056,128]{1,0:T(8,128)S(1)} %bitcast.11, bf16[3,512,512]{2,1,0:T(8,128)(2,1)S(1)} %shard_map.78.table_ref), custom_call_target="tpu_custom_call" | custom-call | flops 134217728 | bytes 2097152 | tf_op jit(solution)/shard_map/pallas_call | solution.py:286
  27.6 2.6 %all-to-all-start.1 = ((f32[32,4,128]{2,1,0:T(4,128)}), f32[32,4,128]{2,1,0:T(4,128)S(1)}, u32[]{:S(2)}, u32[]{:S(2)}) async-start(f32[32,4,128]{2,1,0:T(4,128)} %shard_map.79), calls=%async_computation.1 | async-start | bytes 131072 | tf_op jit(solution)/shard_map/all_to_all | solution.py:287
  30.2 0.4 shard_map.80
  30.5 7.0 %all-to-all-done.1.scores_ref = f32[32,4,128]{2,1,0:T(4,128)S(1)} async-done(((f32[32,4,128]{2,1,0:T(4,128)}), f32[32,4,128]{2,1,0:T(4,128)S(1)}, u32[]{:S(2)}, u32[]{:S(2)}) %all-to-all-start.1) | async-done | bytes 65568 | tf_op jit(solution)/shard_map/all_to_all | solution.py:287
  37.6 3.1 %shard_map.81 = (f32[16,128]{1,0:T(8,128)S(1)}, f32[16,128]{1,0:T(8,128)S(1)}, f32[16,128]{1,0:T(8,128)S(1)}, f32[16,128]{1,0:T(8,128)S(1)}, f32[4]{0:T(128)}) custom-call(f32[32,4,128]{2,1,0:T(4,128)S(1)} %all-to-all-done.1.scores_ref, f32[32,16,128]{2,1,0:T(8,128)S(1)} %get-tuple-element.9.pairs_ref, bf16[256,256]{1,0:T(8,128)(2,1)S(1)} %get-tuple-element.10.query_ref), custom_call_target="tpu_custom_call" | custom-call | flops 268435456 | bytes 2097152 | tf_op jit(solution)/shard_map/pallas_call | solution.py:297
  40.7 0.2 collective-permute-start.2
  40.9 1.1 %collective-permute-done.2 = f32[2,16,128]{2,1,0:T(8,128)S(1)} collective-permute-done((f32[2,16,128]{2,1,0:T(8,128)S(1)}, f32[2,16,128]{2,1,0:T(8,128)S(1)}, u32[]{:S(2)}, u32[]{:S(2)}) %collective-permute-start.2) | collective-permute-done | bytes 16416 | tf_op jit(solution)/shard_map/ppermute | solution.py:248
  42.0 0.5 collective-permute-start.3
  42.4 3.3 %collective-permute-done.3 = f32[2,16,128]{2,1,0:T(8,128)S(1)} collective-permute-done((f32[2,16,128]{2,1,0:T(8,128)S(1)}, f32[2,16,128]{2,1,0:T(8,128)S(1)}, u32[]{:S(2)}, u32[]{:S(2)}) %collective-permute-start.3) | collective-permute-done | bytes 16416 | tf_op jit(solution)/shard_map/ppermute | solution.py:248
  45.7 0.6 %maximum_select_fusion = f32[16,512]{1,0:T(8,128)} fusion(f32[16,256]{1,0:T(8,128)S(1)} %maximum_select_fusion.2, f32[16,256]{1,0:T(8,128)S(1)} %maximum_select_fusion.1, pred[]{:T(512)S(6)} %eq.6), kind=kLoop, calls=%fused_computation | loop fusion | flops 24576 | bytes 65537 | tf_op jit(solution)/shard_map/jit(_where)/select_n | solution.py:315
  (6 shorter events, 0.0 us)
Async XLA Ops:
  0.6 9.6 %copy-start.2 = (s32[128,128]{1,0:T(8,128)S(1)}, s32[128,128]{1,0:T(8,128)}, u32[]{:S(2)}) copy-start(s32[128,128]{1,0:T(8,128)} %codes_ref.1) | copy-start | bytes 196612
  0.6 11.5 %copy-start = (f32[256,1024]{1,0:T(8,128)S(1)}, f32[256,1024]{1,0:T(8,128)}, u32[]{:S(2)}) copy-start(f32[256,1024]{1,0:T(8,128)} %book_ref.1) | copy-start | bytes 3145732
  2.6 23.6 %all-to-all-start = ((f32[32,33,1,128]{3,2,1,0:T(1,128)}), f32[32,33,1,128]{3,2,1,0:T(1,128)S(1)}, u32[]{:S(2)}, u32[]{:S(2)}) async-start(f32[32,33,1,128]{3,2,1,0:T(1,128)} %bitcast.16), calls=%async_computation | async-start | bytes 1081344 | tf_op jit(solution)/shard_map/all_to_all | solution.py:274
  9.9 2.2 %collective-permute-start.1 = (f32[128,1024]{1,0:T(8,128)}, f32[128,1024]{1,0:T(8,128)S(1)}, u32[]{:S(2)}, u32[]{:S(2)}) collective-permute-start(f32[128,1024]{1,0:T(8,128)} %docs_ref.1), channel_id=1, source_target_pairs={{0,1},{1,0},{2,3},{3,2},{4,5},{5,4},{6,7},{7,6},{8,9},{9,8},{10,11... | collective-permute-start | bytes 1572872 | tf_op jit(solution)/shard_map/ppermute | solution.py:248
  10.3 1.8 %collective-permute-start = (s32[128,128]{1,0:T(8,128)S(1)}, s32[128,128]{1,0:T(8,128)S(1)}, u32[]{:S(2)}, u32[]{:S(2)}) collective-permute-start(s32[128,128]{1,0:T(8,128)S(1)} %copy-done.2), channel_id=1, source_target_pairs={{0,1},{1,0},{2,3},{3,2},{4,5},{5,4},{6,7},{7,6},{8,9},{9,8},{10,11... | collective-permute-start | bytes 196616 | tf_op jit(solution)/shard_map/ppermute | solution.py:248
  12.1 1.0 %copy-start.1 = (f32[128,1024]{1,0:T(8,128)S(1)}, f32[128,1024]{1,0:T(8,128)}, u32[]{:S(2)}) copy-start(f32[128,1024]{1,0:T(8,128)} %docs_ref.1) | copy-start | bytes 1572868
  27.6 10.0 %all-to-all-start.1 = ((f32[32,4,128]{2,1,0:T(4,128)}), f32[32,4,128]{2,1,0:T(4,128)S(1)}, u32[]{:S(2)}, u32[]{:S(2)}) async-start(f32[32,4,128]{2,1,0:T(4,128)} %shard_map.79), calls=%async_computation.1 | async-start | bytes 131072 | tf_op jit(solution)/shard_map/all_to_all | solution.py:287
  40.7 1.2 %collective-permute-start.2 = (f32[2,16,128]{2,1,0:T(8,128)S(1)}, f32[2,16,128]{2,1,0:T(8,128)S(1)}, u32[]{:S(2)}, u32[]{:S(2)}) collective-permute-start(f32[2,16,128]{2,1,0:T(8,128)S(1)} %pad_maximum_fusion), channel_id=1, source_target_pairs={{0,1},{1,0},{2,3},{3,2},{4,5},{5,4},{6,7},{7,6},{8,9},{9,8},{10,11... | collective-permute-start | bytes 49160 | tf_op jit(solution)/shard_map/ppermute | solution.py:248
  42.0 3.7 %collective-permute-start.3 = (f32[2,16,128]{2,1,0:T(8,128)S(1)}, f32[2,16,128]{2,1,0:T(8,128)S(1)}, u32[]{:S(2)}, u32[]{:S(2)}) collective-permute-start(f32[2,16,128]{2,1,0:T(8,128)S(1)} %pad_maximum_fusion.1), channel_id=1, source_target_pairs={{0,2},{1,3},{2,0},{3,1},{4,6},{5,7},{6,4},{7,5},{8,10},{9,11},{10,... | collective-permute-start | bytes 49160 | tf_op jit(solution)/shard_map/ppermute | solution.py:248

commit v3 on v2

--- a/solution.py
+++ b/solution.py
@@ -18,6 +18,8 @@
 SPT = LANE // SUB
 QN = 4
 HALF = TILES // 2
+BLOCK = 16
+TOGETHER = 4
 ROWS = HALF * QN + SPT + 1
 
 
@@ -143,24 +145,25 @@
         out_ref[p] = mine
 
 
-def pair_kernel(got_ref, out_ref, query_ref):
+def pair_kernel(got_ref, other_ref, out_ref, query_ref):
     group, dev = place()
-    half = group * 2 + lax.div(lax.rem(dev, 4), 2)
-    first, second, _ = thirds(query_rows(got_ref, half * QN))
-    for rows in (slice(0, LANE), slice(LANE, 2 * LANE)):
-        query_ref[rows, :LANE] = first
-        query_ref[rows, LANE:] = second
+    core, half = lax.rem(dev, 2), group * 2 + lax.div(lax.rem(dev, 4), 2)
     asked = got_ref[pl.ds(ROWS - 1, C, stride=ROWS), :]
     asked = jnp.concatenate([asked, jnp.zeros((LANE - C, LANE), jnp.float32)], axis=0).T
     local = jnp.concatenate([asked[q * C : (q + 1) * C, :C] for q in range(QN)], axis=1)
     local = local.astype(jnp.int32)
-    for o in range(C):
-        index = jnp.broadcast_to(local[o : o + 1, :], (SUB, LANE))
-        for half in range(2):
-            first = o * ROWS + HALF * QN + half * SUB
-            codes = got_ref[first : first + SUB, :]
-            found = jnp.take_along_axis(codes, index, axis=1)
-            out_ref[o, half * SUB : (half + 1) * SUB, :] = found
+    for ref, tile in ((got_ref, core), (other_ref, 1 - core)):
+        first, second, _ = thirds(query_rows(ref, half * QN))
+        for rows in (slice(0, LANE), slice(LANE, 2 * LANE)):
+            query_ref[tile, rows, :LANE] = first
+            query_ref[tile, rows, LANE:] = second
+        for o in range(C):
+            index = jnp.broadcast_to(local[o : o + 1, :], (SUB, LANE))
+            for part in range(SPT // SUB):
+                row = o * ROWS + HALF * QN + part * SUB
+                found = jnp.take_along_axis(ref[row : row + SUB, :], index, axis=1)
+                at = pl.ds(pl.multiple_of(tile * SPT + part * SUB, SUB), SUB)
+                out_ref[o, at, :] = found
 
 
 def log_parts(scores):
@@ -171,11 +174,41 @@
     return powers / total, shifted - jnp.log(total)
 
 
-def gradient_kernel(scores_ref, pairs_ref, query_ref, *refs):
-    own_ref, core_ref, x_ref, both_ref, loss_ref, weight, table = refs
+def block(first, weight, pairs_ref, query_ref, table, out_ref):
+    words = [
+        (iota((SUB, LANE), 0) + (first + v * SUB)).astype(jnp.float32) for v in range(BLOCK // SUB)
+    ]
+
+    @pl.loop(0, 2 * SPT // TOGETHER)
+    def _(step):
+        total = [[jnp.zeros((SUB, LANE), jnp.float32)] * len(words) for _ in range(TOGETHER)]
+        for o in range(C):
+            part = weight[o]
+            for i in range(TOGETHER):
+                row = pairs_ref[o, pl.ds(step * TOGETHER + i, 1), :]
+                code = jnp.broadcast_to(row, (SUB, LANE))
+                for v, word in enumerate(words):
+                    total[i][v] += jnp.where(code == word, part, 0.0)
+        rows = pl.ds(pl.multiple_of(step * (TOGETHER * BLOCK), TOGETHER * BLOCK), TOGETHER * BLOCK)
+        first, second, _ = thirds(jnp.concatenate(sum(total, []), axis=0))
+        table[rows, :LANE] = first
+        table[rows, LANE:] = second
+
+    subspace = lax.div(iota((BLOCK, LANE), 1), SUB)
+    for tile in range(2):
+        base = tile * SPT * BLOCK
+        product = dot(table[base : base + SPT * BLOCK, :], query_ref[tile])
+        product = product[:, :LANE] + product[:, LANE:]
+        result = jnp.zeros((BLOCK, LANE), jnp.float32)
+        for m in range(SPT):
+            rows = product[m * BLOCK : (m + 1) * BLOCK, :]
+            result += jnp.where(subspace == m, rows, 0.0)
+        out_ref[:, tile * LANE : (tile + 1) * LANE] = result
+
+
+def there_kernel(scores_ref, pairs_ref, query_ref, out_ref, weight_ref, loss_ref, table):
     group, dev = place()
     me = group * 16 + dev
-    low = lax.rem(dev, 4)
     odd = lax.rem(iota((C, LANE), 0), 2) == 1
 
     def joined(mine, other):
@@ -192,36 +225,12 @@
         loss_ref[q] = jnp.sum(jnp.where(lanes == q * C + me, loss, 0.0))
     share = soft - teacher
     for o in range(C):
-        weight[o] = jnp.broadcast_to(share[o : o + 1, :], (SUB, LANE))
-    span = 4 * 16
-    first = lax.div(dev, 4) * span
-    words = [(iota((SUB, LANE), 0) + (first + v * SUB)).astype(jnp.float32) for v in range(span // SUB)]
-
-    @pl.loop(0, SPT)
-    def _(m):
-        total = [jnp.zeros((SUB, LANE), jnp.float32)] * len(words)
-        for o in range(C):
-            code = jnp.broadcast_to(pairs_ref[o, pl.ds(m, 1), :], (SUB, LANE))
-            part = weight[o]
-            for v, word in enumerate(words):
-                total[v] += jnp.where(code == word, part, 0.0)
-        rows = pl.ds(pl.multiple_of(m * span, span), span)
-        first, second, _ = thirds(jnp.concatenate(total, axis=0))
-        table[rows, :LANE] = first
-        table[rows, LANE:] = second
-
-    subspace = lax.div(iota((span, LANE), 1), SUB)
-    product = dot(table[...], query_ref[...])
-    product = product[:, :LANE] + product[:, LANE:]
-    result = jnp.zeros((span, LANE), jnp.float32)
-    for m in range(SPT):
-        result += jnp.where(subspace == m, product[m * span : (m + 1) * span, :], 0.0)
-    for i in range(4):
-        block = result[i * 16 : (i + 1) * 16, :]
-        for ref, who in ((own_ref, 0), (core_ref, 1), (x_ref, 2), (both_ref, 3)):
-            @pl.when(low == (i ^ who))
-            def _(ref=ref, block=block):
-                ref[...] = block
+        weight_ref[o] = jnp.broadcast_to(share[o : o + 1, :], (SUB, LANE))
+    block((dev ^ 2) * BLOCK, weight_ref, pairs_ref, query_ref, table, out_ref)
+
+
+def here_kernel(weight_ref, pairs_ref, query_ref, out_ref, table):
+    block(lax.axis_index("dev") * BLOCK, weight_ref, pairs_ref, query_ref, table, out_ref)
 
 
 def vmem(n):
@@ -284,36 +293,34 @@
         1 << 21,
     )(doc_codes, other_codes, codebook, documents, other_docs)
     scores = call(score_kernel, f32(C, 4, LANE), 2, (), vmem(1)[0], 1 << 27, 1 << 21)(got, table)
+    scores, after = lax.optimization_barrier((scores, got))
     all_scores = lax.all_to_all(scores, everyone, split_axis=0, concat_axis=0, tiled=True)
     pairs, columns = call(
         pair_kernel,
-        (f32(C, SPT, LANE), jax.ShapeDtypeStruct((2 * LANE, 2 * LANE), jnp.bfloat16)),
-        1,
+        (f32(C, 2 * SPT, LANE), jax.ShapeDtypeStruct((2, 2 * LANE, 2 * LANE), jnp.bfloat16)),
+        2,
         (),
         tuple(vmem(2)),
         1 << 20,
         1 << 20,
-    )(got)
-    own, core, across, both, query_loss = call(
-        gradient_kernel,
-        (f32(16, LANE),) * 4 + (f32(QN),),
+    )(after, by_xor(after, 1, owners))
+    built = [pltpu.VMEM((2 * SPT * BLOCK, 2 * LANE), jnp.bfloat16)]
+    there, weight, query_loss = call(
+        there_kernel,
+        (f32(BLOCK, 2 * LANE), f32(C, SUB, LANE), f32(QN)),
         3,
-        [pltpu.VMEM((C, SUB, LANE), jnp.float32), pltpu.VMEM((SPT * 64, 2 * LANE), jnp.bfloat16)],
-        tuple(vmem(4)) + (pl.BlockSpec(memory_space=pltpu.SMEM),),
-        1 << 28,
+        built,
+        tuple(vmem(2)) + (pl.BlockSpec(memory_space=pltpu.SMEM),),
+        1 << 27,
         1 << 21,
     )(all_scores, pairs, columns)
-    near = by_xor(jnp.stack([core, both]), 1, owners)
-    far = by_xor(jnp.stack([across, near[1]]), 2, owners)
-    dev = lax.axis_index("dev")
-    odd_core, odd_x = lax.rem(dev, 2) == 1, lax.rem(lax.div(dev, 2), 2) == 1
-
-    def pair(mine, other):
-        return jnp.where(odd_core, jnp.concatenate([other, mine], 1), jnp.concatenate([mine, other], 1))
-
-    here, there = pair(own, near[0]), pair(far[0], far[1])
+    far = by_xor(there, 2, owners)
+    here = call(here_kernel, f32(BLOCK, 2 * LANE), 3, built, vmem(1)[0], 1 << 27, 1 << 21)(
+        weight, pairs, columns
+    )
+    second = lax.rem(lax.div(lax.axis_index("dev"), 2), 2) == 1
     gradient = jnp.where(
-        odd_x, jnp.concatenate([there, here], 1), jnp.concatenate([here, there], 1)
+        second, jnp.concatenate([far, here], 1), jnp.concatenate([here, far], 1)
     )
     return gradient, query_loss
 

time: 46.6 us -> 44.1 us (0.946)
  waiting for transfers between devices: 25 us -> 22.5 us
    ppermute x4, waiting for transfers between devices: 5.95 us -> 3.63 us  [by_xor(): return lax.ppermute(value, 'dev', [(i, i ^ bits) for i in range(count)])]
    pallas_call x2 -> x3, Pallas kernels: 3.52 us -> 3.58 us  [the longest x1 1.77 us: shards_once(): call(there_kernel, (f32(BLOCK, 2 * LANE), f32(C, SUB, LANE), f32(QN)), 3,...]
  transfers between devices with their start and end apart: 6 -> 6, of which waited for: 6 -> 5; matrix products, arithmetic and copies ran while one was open for 0% -> 0% of each run, Pallas kernels for 3% -> 6%
where the time goes in v3:
time: 44.1 us; the launch traced here: 43.8 us
  waiting for transfers between devices  22.5 us (51%)
  starting transfers between devices  10.9 us (25%)
  Pallas kernels  7.98 us (18%)
  local copies, waits for them, and re-layouts  1.05 us (2%)
  between operations  0.7 us (2%)
  other arithmetic  0.62 us (1%)
    all_to_all x1, waiting for transfers between devices, shards_once(): lax.all_to_all(sent.reshape(C, ROWS, 1, LANE), everyone, split_axis=0, co...  12 us
    all_to_all x1, starting transfers between devices, shards_once(): lax.all_to_all(sent.reshape(C, ROWS, 1, LANE), everyone, split_axis=0, co...  7.3 us
    all_to_all x1, waiting for transfers between devices, shards_once(): lax.all_to_all(scores, everyone, split_axis=0, concat_axis=0, tiled=True)  6.84 us
    ppermute x4, waiting for transfers between devices, by_xor(): return lax.ppermute(value, 'dev', [(i, i ^ bits) for i in range(count)])  3.63 us
    all_to_all x1, starting transfers between devices, shards_once(): lax.all_to_all(scores, everyone, split_axis=0, concat_axis=0, tiled=True)  2.54 us
    pallas_call x1, Pallas kernels, shards_once(): call(pack_kernel, f32(C * ROWS, LANE), 4, [pltpu.VMEM((QN, D), jnp.float3...  1.98 us
    pallas_call x1, Pallas kernels, shards_once(): call(there_kernel, (f32(BLOCK, 2 * LANE), f32(C, SUB, LANE), f32(QN)), 3,...  1.77 us
    pallas_call x1, Pallas kernels, shards_once(): call(score_kernel, f32(C, 4, LANE), 2, (), vmem(1)[0], 1 << 27, 1 << 21)  1.39 us
  transfers between devices with their start and end apart: 6, of which 5 were waited for; matrix products, arithmetic and copies ran while one was open for 0% of the time, Pallas kernels for 6%

profile of v3, /device:TPU:0, one launch (start us, length us, event | category | flops | bytes accessed | tf_op | source)
XLA Modules:
  0.0 43.8 jit_solution(116315565045885082)
XLA Ops:
  0.6 0.0 copy-start.2
  0.6 0.0 copy-start
  0.7 2.0 %shard_map.77 = f32[1056,128]{1,0:T(8,128)} custom-call(f32[4,1024]{1,0:T(4,128)} %refs_0_.1, s32[128,128]{1,0:T(8,128)} %codes_ref.1, s32[4,32]{1,0:T(4,128)} %refs_2_.1, s32[4,32]{1,0:T(4,128)} %refs_3_.1), custom_call_target="tpu_custom_call" | custom-call | bytes 1048576 | tf_op jit(solution)/shard_map/pallas_call | solution.py:265
  2.6 7.3 %all-to-all-start = ((f32[32,33,1,128]{3,2,1,0:T(1,128)}), f32[32,33,1,128]{3,2,1,0:T(1,128)S(1)}, u32[]{:S(2)}, u32[]{:S(2)}) async-start(f32[32,33,1,128]{3,2,1,0:T(1,128)} %bitcast.5), calls=%async_computation | async-start | bytes 1081344 | tf_op jit(solution)/shard_map/all_to_all | solution.py:283
  10.0 0.3 collective-permute-start.1
  10.3 0.0 copy-done.2
  10.3 0.3 collective-permute-start
  10.5 1.5 %collective-permute-done.other_ref = s32[128,128]{1,0:T(8,128)S(1)} collective-permute-done((s32[128,128]{1,0:T(8,128)S(1)}, s32[128,128]{1,0:T(8,128)S(1)}, u32[]{:S(2)}, u32[]{:S(2)}) %collective-permute-start) | collective-permute-done | bytes 65568 | tf_op jit(solution)/shard_map/ppermute | solution.py:257
  12.0 0.1 collective-permute-done.1.other_docs_ref
  12.1 0.0 copy-done
  12.1 0.0 copy-start.1
  12.1 1.0 %copy-done.1 = f32[128,1024]{1,0:T(8,128)S(1)} copy-done((f32[128,1024]{1,0:T(8,128)S(1)}, f32[128,1024]{1,0:T(8,128)}, u32[]{:S(2)}) %copy-start.1) | copy-done | bytes 524312
  13.2 1.0 %shard_map.78.table_ref = bf16[3,512,512]{2,1,0:T(8,128)(2,1)S(1)} custom-call(s32[128,128]{1,0:T(8,128)S(1)} %copy-done.2, s32[128,128]{1,0:T(8,128)S(1)} %collective-permute-done.other_ref, f32[256,1024]{1,0:T(8,128)S(1)} %copy-done, f32[128,1024]{1,0:T(8,128)S(1)} %copy-done.1, f32[128,1024]{1,0:T(8,128)S(1)} %collective-permute-done.1.other_docs_ref), custom_call_target="tpu_custom_call" | custom-call | flops 4194304 | bytes 2097152 | tf_op jit(solution)/shard_map/pallas_call | solution.py:286
  14.2 12.0 %all-to-all-done = f32[32,33,1,128]{3,2,1,0:T(1,128)S(1)} async-done(((f32[32,33,1,128]{3,2,1,0:T(1,128)}), f32[32,33,1,128]{3,2,1,0:T(1,128)S(1)}, u32[]{:S(2)}, u32[]{:S(2)}) %all-to-all-start) | async-done | bytes 540704 | tf_op jit(solution)/shard_map/all_to_all | solution.py:283
  26.2 1.4 %shard_map.79 = f32[32,4,128]{2,1,0:T(4,128)} custom-call(f32[1056,128]{1,0:T(8,128)S(1)} %bitcast.2, bf16[3,512,512]{2,1,0:T(8,128)(2,1)S(1)} %shard_map.78.table_ref), custom_call_target="tpu_custom_call" | custom-call | flops 134217728 | bytes 2097152 | tf_op jit(solution)/shard_map/pallas_call | solution.py:295
  27.6 0.0 collective-permute-start.2
  27.6 2.5 %all-to-all-start.1 = ((f32[32,4,128]{2,1,0:T(4,128)}), f32[32,4,128]{2,1,0:T(4,128)S(1)}, u32[]{:S(2)}, u32[]{:S(2)}) async-start(f32[32,4,128]{2,1,0:T(4,128)} %shard_map.79), calls=%async_computation.1 | async-start | bytes 131072 | tf_op jit(solution)/shard_map/all_to_all | solution.py:297
  30.2 0.0 collective-permute-done.2.other_ref
  30.2 0.6 %shard_map.80 = (f32[32,32,128]{2,1,0:T(8,128)S(1)}, bf16[2,256,256]{2,1,0:T(8,128)(2,1)S(1)}) custom-call(f32[1056,128]{1,0:T(8,128)S(1)} %bitcast.4, f32[1056,128]{1,0:T(8,128)S(1)} %collective-permute-done.2.other_ref), custom_call_target="tpu_custom_call" | custom-call | flops 1048576 | bytes 1048576 | tf_op jit(solution)/shard_map/pallas_call | solution.py:298
  30.7 6.8 %all-to-all-done.1.scores_ref = f32[32,4,128]{2,1,0:T(4,128)S(1)} async-done(((f32[32,4,128]{2,1,0:T(4,128)}), f32[32,4,128]{2,1,0:T(4,128)S(1)}, u32[]{:S(2)}, u32[]{:S(2)}) %all-to-all-start.1) | async-done | bytes 65568 | tf_op jit(solution)/shard_map/all_to_all | solution.py:297
  37.6 1.8 %shard_map.81 = (f32[16,256]{1,0:T(8,128)S(1)}, f32[32,8,128]{2,1,0:T(8,128)S(1)}, f32[4]{0:T(128)}) custom-call(f32[32,4,128]{2,1,0:T(4,128)S(1)} %all-to-all-done.1.scores_ref, f32[32,32,128]{2,1,0:T(8,128)S(1)} %get-tuple-element.11.pairs_ref, bf16[2,256,256]{2,1,0:T(8,128)(2,1)S(1)} %get-tuple-element.12.query_ref), custom_call_target="tpu_custom_call" | custom-call | flops 134217728 | bytes 2097152 | tf_op jit(solution)/shard_map/pallas_call | solution.py:308
  39.4 0.5 %collective-permute-start.3 = (f32[16,256]{1,0:T(8,128)S(1)}, f32[16,256]{1,0:T(8,128)S(1)}, u32[]{:S(2)}, u32[]{:S(2)}) collective-permute-start(f32[16,256]{1,0:T(8,128)S(1)} %get-tuple-element.13), channel_id=1, source_target_pairs={{0,2},{1,3},{2,0},{3,1},{4,6},{5,7},{6,4},{7,5},{8,10},{9,11},{10,... | collective-permute-start | bytes 49160 | tf_op jit(solution)/shard_map/ppermute | solution.py:257
  39.9 1.3 %shard_map.82 = f32[16,256]{1,0:T(8,128)S(1)} custom-call(f32[32,8,128]{2,1,0:T(8,128)S(1)} %get-tuple-element.14.weight_ref, f32[32,32,128]{2,1,0:T(8,128)S(1)} %get-tuple-element.11.pairs_ref, bf16[2,256,256]{2,1,0:T(8,128)(2,1)S(1)} %get-tuple-element.12.query_ref), custom_call_target="tpu_custom_call" | custom-call | flops 134217728 | bytes 2097152 | tf_op jit(solution)/shard_map/pallas_call | solution.py:318
  41.1 2.0 %collective-permute-done.3 = f32[16,256]{1,0:T(8,128)S(1)} collective-permute-done((f32[16,256]{1,0:T(8,128)S(1)}, f32[16,256]{1,0:T(8,128)S(1)}, u32[]{:S(2)}, u32[]{:S(2)}) %collective-permute-start.3) | collective-permute-done | bytes 16416 | tf_op jit(solution)/shard_map/ppermute | solution.py:257
  43.2 0.6 %maximum_select_fusion = f32[16,512]{1,0:T(8,128)} fusion(f32[16,256]{1,0:T(8,128)S(1)} %shard_map.82, f32[16,256]{1,0:T(8,128)S(1)} %collective-permute-done.3, pred[]{:T(512)S(6)} %eq.3), kind=kLoop, calls=%fused_computation | loop fusion | flops 24576 | bytes 65537 | tf_op jit(solution)/shard_map/jit(_where)/select_n | solution.py:322
Async XLA Ops:
  0.6 9.6 %copy-start.2 = (s32[128,128]{1,0:T(8,128)S(1)}, s32[128,128]{1,0:T(8,128)}, u32[]{:S(2)}) copy-start(s32[128,128]{1,0:T(8,128)} %codes_ref.1) | copy-start | bytes 196612
  0.6 11.5 %copy-start = (f32[256,1024]{1,0:T(8,128)S(1)}, f32[256,1024]{1,0:T(8,128)}, u32[]{:S(2)}) copy-start(f32[256,1024]{1,0:T(8,128)} %book_ref.1) | copy-start | bytes 3145732
  2.6 23.6 %all-to-all-start = ((f32[32,33,1,128]{3,2,1,0:T(1,128)}), f32[32,33,1,128]{3,2,1,0:T(1,128)S(1)}, u32[]{:S(2)}, u32[]{:S(2)}) async-start(f32[32,33,1,128]{3,2,1,0:T(1,128)} %bitcast.5), calls=%async_computation | async-start | bytes 1081344 | tf_op jit(solution)/shard_map/all_to_all | solution.py:283
  10.0 2.2 %collective-permute-start.1 = (f32[128,1024]{1,0:T(8,128)}, f32[128,1024]{1,0:T(8,128)S(1)}, u32[]{:S(2)}, u32[]{:S(2)}) collective-permute-start(f32[128,1024]{1,0:T(8,128)} %docs_ref.1), channel_id=1, source_target_pairs={{0,1},{1,0},{2,3},{3,2},{4,5},{5,4},{6,7},{7,6},{8,9},{9,8},{10,11... | collective-permute-start | bytes 1572872 | tf_op jit(solution)/shard_map/ppermute | solution.py:257
  10.3 1.8 %collective-permute-start = (s32[128,128]{1,0:T(8,128)S(1)}, s32[128,128]{1,0:T(8,128)S(1)}, u32[]{:S(2)}, u32[]{:S(2)}) collective-permute-start(s32[128,128]{1,0:T(8,128)S(1)} %copy-done.2), channel_id=1, source_target_pairs={{0,1},{1,0},{2,3},{3,2},{4,5},{5,4},{6,7},{7,6},{8,9},{9,8},{10,11... | collective-permute-start | bytes 196616 | tf_op jit(solution)/shard_map/ppermute | solution.py:257
  12.1 1.0 %copy-start.1 = (f32[128,1024]{1,0:T(8,128)S(1)}, f32[128,1024]{1,0:T(8,128)}, u32[]{:S(2)}) copy-start(f32[128,1024]{1,0:T(8,128)} %docs_ref.1) | copy-start | bytes 1572868
  27.6 2.6 %collective-permute-start.2 = (f32[1056,128]{1,0:T(8,128)S(1)}, f32[1056,128]{1,0:T(8,128)S(1)}, u32[]{:S(2)}, u32[]{:S(2)}) collective-permute-start(f32[1056,128]{1,0:T(8,128)S(1)} %bitcast.3), channel_id=1, source_target_pairs={{0,1},{1,0},{2,3},{3,2},{4,5},{5,4},{6,7},{7,6},{8,9},{9,8},{10,11... | collective-permute-start | bytes 1622024 | tf_op jit(solution)/shard_map/ppermute | solution.py:257
  27.6 10.0 %all-to-all-start.1 = ((f32[32,4,128]{2,1,0:T(4,128)}), f32[32,4,128]{2,1,0:T(4,128)S(1)}, u32[]{:S(2)}, u32[]{:S(2)}) async-start(f32[32,4,128]{2,1,0:T(4,128)} %shard_map.79), calls=%async_computation.1 | async-start | bytes 131072 | tf_op jit(solution)/shard_map/all_to_all | solution.py:297
  39.4 3.8 %collective-permute-start.3 = (f32[16,256]{1,0:T(8,128)S(1)}, f32[16,256]{1,0:T(8,128)S(1)}, u32[]{:S(2)}, u32[]{:S(2)}) collective-permute-start(f32[16,256]{1,0:T(8,128)S(1)} %get-tuple-element.13), channel_id=1, source_target_pairs={{0,2},{1,3},{2,0},{3,1},{4,6},{5,7},{6,4},{7,5},{8,10},{9,11},{10,... | collective-permute-start | bytes 49160 | tf_op jit(solution)/shard_map/ppermute | solution.py:257

commit v4 on v3

--- a/solution.py
+++ b/solution.py
@@ -20,7 +20,7 @@
 HALF = TILES // 2
 BLOCK = 16
 TOGETHER = 4
-ROWS = HALF * QN + SPT + 1
+ROWS = HALF * QN + SUB + 1
 
 
 def iota(shape, axis):
@@ -72,8 +72,9 @@
             t = 2 * i + core
             out_ref[base + i * QN : base + (i + 1) * QN, :] = q_ref[:, t * LANE : (t + 1) * LANE]
         first = base + HALF * QN
-        out_ref[first : first + SPT, :] = codes_t[tile * SPT : (tile + 1) * SPT, :]
-        out_ref[first + SPT : first + SPT + 1, :] = row
+        start = tile * SPT + p // 4 % 2 * SUB
+        out_ref[first : first + SUB, :] = codes_t[start : start + SUB, :]
+        out_ref[first + SUB : first + SUB + 1, :] = row
 
 
 def owner_kernel(codes_ref, other_ref, book_ref, docs_ref, other_docs_ref, out_ref, book_t, codes_t):
@@ -109,16 +110,18 @@
     return jnp.concatenate([got_ref[pl.ds(row + q, C, stride=ROWS), :] for q in range(QN)], axis=0)
 
 
-def score_kernel(got_ref, table_ref, out_ref):
+def score_kernel(got_ref, table_ref, out_ref, codes_ref):
     group, dev = place()
     me = group * 16 + dev
     core = lax.rem(dev, 2)
     query = jnp.concatenate([query_rows(got_ref, i * QN) for i in range(HALF)], axis=1)
     q0, q1, q2 = thirds(query)
     t0, t1, t2 = table_ref[0], table_ref[1], table_ref[2]
-    scores = dot(q0, t2) + dot(q2, t0) + dot(q1, t1)
-    scores = scores + (dot(q0, t1) + dot(q1, t0))
-    scores = scores + dot(q0, t0)
+    by_first = dot(jnp.concatenate([q0, q1, q2], axis=0), t0)
+    by_second = dot(jnp.concatenate([q0, q1], axis=0), t1)
+    scores = dot(q0, t2) + by_first[2 * LANE :] + by_second[LANE:]
+    scores = scores + (by_second[:LANE] + by_first[LANE : 2 * LANE])
+    scores = scores + by_first[:LANE]
     asked = got_ref[pl.ds(ROWS - 1, C, stride=ROWS), :]
     lanes = iota((C, LANE), 1)
     wide = iota((LANE, LANE), 1)
@@ -143,11 +146,14 @@
     mine = jnp.concatenate(rows, axis=0)
     for p in range(C):
         out_ref[p] = mine
-
-
-def pair_kernel(got_ref, other_ref, out_ref, query_ref):
+        first = p * ROWS + HALF * QN
+        codes_ref[p] = got_ref[first : first + SUB, :]
+
+
+def pair_kernel(got_ref, codes_ref, more_ref, other_ref, other_more_ref, out_ref, query_ref):
     group, dev = place()
     core, half = lax.rem(dev, 2), group * 2 + lax.div(lax.rem(dev, 4), 2)
+    own = lax.rem(lax.div(dev, 4), 2)
     asked = got_ref[pl.ds(ROWS - 1, C, stride=ROWS), :]
     asked = jnp.concatenate([asked, jnp.zeros((LANE - C, LANE), jnp.float32)], axis=0).T
     local = jnp.concatenate([asked[q * C : (q + 1) * C, :C] for q in range(QN)], axis=1)
@@ -157,13 +163,17 @@
         for rows in (slice(0, LANE), slice(LANE, 2 * LANE)):
             query_ref[tile, rows, :LANE] = first
             query_ref[tile, rows, LANE:] = second
-        for o in range(C):
-            index = jnp.broadcast_to(local[o : o + 1, :], (SUB, LANE))
-            for part in range(SPT // SUB):
-                row = o * ROWS + HALF * QN + part * SUB
-                found = jnp.take_along_axis(ref[row : row + SUB, :], index, axis=1)
-                at = pl.ds(pl.multiple_of(tile * SPT + part * SUB, SUB), SUB)
-                out_ref[o, at, :] = found
+    at = [
+        pl.ds(pl.multiple_of(tile * SPT + part * SUB, SUB), SUB)
+        for tile in (core, 1 - core)
+        for part in (own, 1 - own)
+    ]
+    for o in range(C):
+        index = jnp.broadcast_to(local[o : o + 1, :], (SUB, LANE))
+        row = o * ROWS + HALF * QN
+        found = (codes_ref[o], more_ref[o], other_ref[row : row + SUB, :], other_more_ref[o])
+        for rows, value in zip(at, found):
+            out_ref[o, rows, :] = jnp.take_along_axis(value, index, axis=1)
 
 
 def log_parts(scores):
@@ -207,8 +217,7 @@
 
 
 def there_kernel(scores_ref, pairs_ref, query_ref, out_ref, weight_ref, loss_ref, table):
-    group, dev = place()
-    me = group * 16 + dev
+    dev = lax.axis_index("dev")
     odd = lax.rem(iota((C, LANE), 0), 2) == 1
 
     def joined(mine, other):
@@ -220,16 +229,19 @@
     teacher, log_teacher = log_parts(exact)
     soft, log_soft = log_parts(student)
     loss = jnp.sum(teacher * (log_teacher - log_soft), axis=0, keepdims=True)
-    lanes = iota((1, LANE), 1)
-    for q in range(QN):
-        loss_ref[q] = jnp.sum(jnp.where(lanes == q * C + me, loss, 0.0))
+    loss_ref[...] = loss
     share = soft - teacher
     for o in range(C):
         weight_ref[o] = jnp.broadcast_to(share[o : o + 1, :], (SUB, LANE))
     block((dev ^ 2) * BLOCK, weight_ref, pairs_ref, query_ref, table, out_ref)
 
 
-def here_kernel(weight_ref, pairs_ref, query_ref, out_ref, table):
+def here_kernel(weight_ref, loss_ref, pairs_ref, query_ref, out_ref, own_loss_ref, table):
+    group, dev = place()
+    lanes = iota((1, LANE), 1)
+    for q in range(QN):
+        mine = lanes == q * C + group * 16 + dev
+        own_loss_ref[q] = jnp.sum(jnp.where(mine, loss_ref[...], 0.0))
     block(lax.axis_index("dev") * BLOCK, weight_ref, pairs_ref, query_ref, table, out_ref)
 
 
@@ -292,32 +304,41 @@
         1 << 22,
         1 << 21,
     )(doc_codes, other_codes, codebook, documents, other_docs)
-    scores = call(score_kernel, f32(C, 4, LANE), 2, (), vmem(1)[0], 1 << 27, 1 << 21)(got, table)
+    scores, codes = call(
+        score_kernel, (f32(C, 4, LANE), f32(C, SUB, LANE)), 2, (), tuple(vmem(2)), 1 << 27, 1 << 21
+    )(got, table)
+    more = by_xor(codes, 4, owners)
     scores, after = lax.optimization_barrier((scores, got))
     all_scores = lax.all_to_all(scores, everyone, split_axis=0, concat_axis=0, tiled=True)
     pairs, columns = call(
         pair_kernel,
         (f32(C, 2 * SPT, LANE), jax.ShapeDtypeStruct((2, 2 * LANE, 2 * LANE), jnp.bfloat16)),
-        2,
+        5,
         (),
         tuple(vmem(2)),
         1 << 20,
         1 << 20,
-    )(after, by_xor(after, 1, owners))
+    )(after, codes, more, by_xor(after, 1, owners), by_xor(codes, 5, owners))
     built = [pltpu.VMEM((2 * SPT * BLOCK, 2 * LANE), jnp.bfloat16)]
-    there, weight, query_loss = call(
+    there, weight, losses = call(
         there_kernel,
-        (f32(BLOCK, 2 * LANE), f32(C, SUB, LANE), f32(QN)),
+        (f32(BLOCK, 2 * LANE), f32(C, SUB, LANE), f32(1, LANE)),
         3,
         built,
-        tuple(vmem(2)) + (pl.BlockSpec(memory_space=pltpu.SMEM),),
+        tuple(vmem(3)),
         1 << 27,
         1 << 21,
     )(all_scores, pairs, columns)
     far = by_xor(there, 2, owners)
-    here = call(here_kernel, f32(BLOCK, 2 * LANE), 3, built, vmem(1)[0], 1 << 27, 1 << 21)(
-        weight, pairs, columns
-    )
+    here, query_loss = call(
+        here_kernel,
+        (f32(BLOCK, 2 * LANE), f32(QN)),
+        4,
+        built,
+        (vmem(1)[0], pl.BlockSpec(memory_space=pltpu.SMEM)),
+        1 << 27,
+        1 << 21,
+    )(weight, losses, pairs, columns)
     second = lax.rem(lax.div(lax.axis_index("dev"), 2), 2) == 1
     gradient = jnp.where(
         second, jnp.concatenate([far, here], 1), jnp.concatenate([here, far], 1)

time: 44.1 us -> 42.6 us (0.966)
  waiting for transfers between devices: 22.5 us -> 18.5 us
  starting transfers between devices: 10.9 us -> 12.8 us
  local copies, waits for them, and re-layouts: 1.05 us -> 1.88 us
    all_to_all x1, waiting for transfers between devices: 6.84 us -> 2.89 us  [shards_once(): lax.all_to_all(scores, everyone, split_axis=0, concat_axis=0, tiled=True)]
    all_to_all x1, waiting for transfers between devices: 12 us -> 8.26 us  [shards_once(): lax.all_to_all(sent.reshape(C, ROWS, 1, LANE), everyone, split_axis=0, co...]
    ppermute x4 -> x6, waiting for transfers between devices: 3.63 us -> 7.34 us  [by_xor(): return lax.ppermute(value, 'dev', [(i, i ^ bits) for i in range(count)])]
    ppermute x4 -> x6, starting transfers between devices: 1.1 us -> 2.95 us  [by_xor(): return lax.ppermute(value, 'dev', [(i, i ^ bits) for i in range(count)])]
    unnamed x6, local copies, waits for them, and re-layouts: 1.05 us -> 1.88 us
  transfers between devices with their start and end apart: 6 -> 8, of which waited for: 5 -> 6; matrix products, arithmetic and copies ran while one was open for 0% -> 0% of each run, Pallas kernels for 6% -> 8%
where the time goes in v4:
time: 42.6 us; the launch traced here: 42.3 us
  waiting for transfers between devices  18.5 us (43%)
  starting transfers between devices  12.8 us (30%)
  Pallas kernels  7.77 us (18%)
  local copies, waits for them, and re-layouts  1.88 us (4%)
  between operations  0.7 us (2%)
  other arithmetic  0.62 us (1%)
    all_to_all x1, waiting for transfers between devices, shards_once(): lax.all_to_all(sent.reshape(C, ROWS, 1, LANE), everyone, split_axis=0, co...  8.26 us
    ppermute x6, waiting for transfers between devices, by_xor(): return lax.ppermute(value, 'dev', [(i, i ^ bits) for i in range(count)])  7.34 us
    all_to_all x1, starting transfers between devices, shards_once(): lax.all_to_all(sent.reshape(C, ROWS, 1, LANE), everyone, split_axis=0, co...  7.3 us
    ppermute x6, starting transfers between devices, by_xor(): return lax.ppermute(value, 'dev', [(i, i ^ bits) for i in range(count)])  2.95 us
    all_to_all x1, waiting for transfers between devices, shards_once(): lax.all_to_all(scores, everyone, split_axis=0, concat_axis=0, tiled=True)  2.89 us
    all_to_all x1, starting transfers between devices, shards_once(): lax.all_to_all(scores, everyone, split_axis=0, concat_axis=0, tiled=True)  2.56 us
    pallas_call x1, Pallas kernels, shards_once(): call(pack_kernel, f32(C * ROWS, LANE), 4, [pltpu.VMEM((QN, D), jnp.float3...  1.93 us
    unnamed x6, local copies, waits for them, and re-layouts  1.88 us
  transfers between devices with their start and end apart: 8, of which 6 were waited for; matrix products, arithmetic and copies ran while one was open for 0% of the time, Pallas kernels for 8%

profile of v4, /device:TPU:0, one launch (start us, length us, event | category | flops | bytes accessed | tf_op | source)
XLA Modules:
  0.0 42.3 jit_solution(16464225877944961308)
XLA Ops:
  0.6 0.0 copy-start
  0.6 1.9 %shard_map.77 = f32[800,128]{1,0:T(8,128)} custom-call(f32[4,1024]{1,0:T(4,128)} %refs_0_.1, s32[128,128]{1,0:T(8,128)} %codes_ref.1, s32[4,32]{1,0:T(4,128)} %refs_2_.1, s32[4,32]{1,0:T(4,128)} %refs_3_.1), custom_call_target="tpu_custom_call" | custom-call | bytes 1048576 | tf_op jit(solution)/shard_map/pallas_call | solution.py:277
  2.6 7.3 %all-to-all-start = ((f32[32,25,1,128]{3,2,1,0:T(1,128)}), f32[32,25,1,128]{3,2,1,0:T(1,128)S(1)}, u32[]{:S(2)}, u32[]{:S(2)}) async-start(f32[32,25,1,128]{3,2,1,0:T(1,128)} %bitcast.5), calls=%async_computation | async-start | bytes 819200 | tf_op jit(solution)/shard_map/all_to_all | solution.py:295
  9.9 0.3 collective-permute-start.1
  10.2 0.3 collective-permute-start
  10.5 1.7 %collective-permute-done.other_ref = s32[128,128]{1,0:T(8,128)S(1)} collective-permute-done((s32[128,128]{1,0:T(8,128)}, s32[128,128]{1,0:T(8,128)S(1)}, u32[]{:S(2)}, u32[]{:S(2)}) %collective-permute-start) | collective-permute-done | bytes 65568 | tf_op jit(solution)/shard_map/ppermute | solution.py:269
  12.2 0.0 collective-permute-done.1.other_docs_ref
  12.2 0.0 copy-done
  12.2 0.0 copy-start.1
  12.2 1.0 %copy-done.1 = f32[128,1024]{1,0:T(8,128)S(1)} copy-done((f32[128,1024]{1,0:T(8,128)S(1)}, f32[128,1024]{1,0:T(8,128)}, u32[]{:S(2)}) %copy-start.1) | copy-done | bytes 524312
  13.2 0.0 copy-start.2
  13.2 0.8 %copy-done.2 = s32[128,128]{1,0:T(8,128)S(1)} copy-done((s32[128,128]{1,0:T(8,128)S(1)}, s32[128,128]{1,0:T(8,128)}, u32[]{:S(2)}) %copy-start.2) | copy-done | bytes 65560
  14.1 1.0 %shard_map.78.table_ref = bf16[3,512,512]{2,1,0:T(8,128)(2,1)S(1)} custom-call(s32[128,128]{1,0:T(8,128)S(1)} %copy-done.2, s32[128,128]{1,0:T(8,128)S(1)} %collective-permute-done.other_ref, f32[256,1024]{1,0:T(8,128)S(1)} %copy-done, f32[128,1024]{1,0:T(8,128)S(1)} %copy-done.1, f32[128,1024]{1,0:T(8,128)S(1)} %collective-permute-done.1.other_docs_ref), custom_call_target="tpu_custom_call" | custom-call | flops 4194304 | bytes 2097152 | tf_op jit(solution)/shard_map/pallas_call | solution.py:298
  15.1 8.3 %all-to-all-done = f32[32,25,1,128]{3,2,1,0:T(1,128)S(1)} async-done(((f32[32,25,1,128]{3,2,1,0:T(1,128)}), f32[32,25,1,128]{3,2,1,0:T(1,128)S(1)}, u32[]{:S(2)}, u32[]{:S(2)}) %all-to-all-start) | async-done | bytes 409632 | tf_op jit(solution)/shard_map/all_to_all | solution.py:295
  23.3 1.3 %shard_map.79 = (f32[32,4,128]{2,1,0:T(4,128)}, f32[32,8,128]{2,1,0:T(8,128)S(1)}) custom-call(f32[800,128]{1,0:T(8,128)S(1)} %bitcast.2, bf16[3,512,512]{2,1,0:T(8,128)(2,1)S(1)} %shard_map.78.table_ref), custom_call_target="tpu_custom_call" | custom-call | flops 134217728 | bytes 2097152 | tf_op jit(solution)/shard_map/pallas_call | solution.py:307
  24.7 0.0 collective-permute-start.3
  24.7 0.9 %collective-permute-start.2 = (f32[32,8,128]{2,1,0:T(8,128)S(1)}, f32[32,8,128]{2,1,0:T(8,128)S(1)}, u32[]{:S(2)}, u32[]{:S(2)}) collective-permute-start(f32[32,8,128]{2,1,0:T(8,128)S(1)} %get-tuple-element.16.codes_ref), channel_id=1, source_target_pairs={{0,4},{1,5},{2,6},{3,7},{4,0},{5,1},{6,2},{7,3},{8,12},{9,13},{10,... | collective-permute-start | bytes 393224 | tf_op jit(solution)/shard_map/ppermute | solution.py:269
  25.5 1.0 %collective-permute-start.4 = (f32[32,8,128]{2,1,0:T(8,128)S(1)}, f32[32,8,128]{2,1,0:T(8,128)S(1)}, u32[]{:S(2)}, u32[]{:S(2)}) collective-permute-start(f32[32,8,128]{2,1,0:T(8,128)S(1)} %get-tuple-element.16.codes_ref), channel_id=1, source_target_pairs={{0,5},{1,4},{2,7},{3,6},{4,1},{5,0},{6,3},{7,2},{8,13},{9,12},{10,... | collective-permute-start | bytes 393224 | tf_op jit(solution)/shard_map/ppermute | solution.py:269
  26.5 2.6 %all-to-all-start.1 = ((f32[32,4,128]{2,1,0:T(4,128)}), f32[32,4,128]{2,1,0:T(4,128)S(1)}, u32[]{:S(2)}, u32[]{:S(2)}) async-start(f32[32,4,128]{2,1,0:T(4,128)} %get-tuple-element.14), calls=%async_computation.1 | async-start | bytes 131072 | tf_op jit(solution)/shard_map/all_to_all | solution.py:312
  29.1 1.9 %collective-permute-done.2.more_ref = f32[32,8,128]{2,1,0:T(8,128)S(1)} collective-permute-done((f32[32,8,128]{2,1,0:T(8,128)S(1)}, f32[32,8,128]{2,1,0:T(8,128)S(1)}, u32[]{:S(2)}, u32[]{:S(2)}) %collective-permute-start.2) | collective-permute-done | bytes 131104 | tf_op jit(solution)/shard_map/ppermute | solution.py:269
  31.0 2.2 %collective-permute-done.4.other_more_ref = f32[32,8,128]{2,1,0:T(8,128)S(1)} collective-permute-done((f32[32,8,128]{2,1,0:T(8,128)S(1)}, f32[32,8,128]{2,1,0:T(8,128)S(1)}, u32[]{:S(2)}, u32[]{:S(2)}) %collective-permute-start.4) | collective-permute-done | bytes 131104 | tf_op jit(solution)/shard_map/ppermute | solution.py:269
  33.1 0.0 collective-permute-done.3.other_ref
  33.1 0.5 %shard_map.80 = (f32[32,32,128]{2,1,0:T(8,128)S(1)}, bf16[2,256,256]{2,1,0:T(8,128)(2,1)S(1)}) custom-call(f32[800,128]{1,0:T(8,128)S(1)} %bitcast.4, f32[32,8,128]{2,1,0:T(8,128)S(1)} %get-tuple-element.16.codes_ref, f32[32,8,128]{2,1,0:T(8,128)S(1)} %collective-permute-done.2.more_ref, f32[800,128]{1,0:T(8,128)S(1)} %collective-permute-done.3.other_ref, ...), custom_call_target="tpu_custom_call" | custom-call | flops 1048576 | bytes 1048576 | tf_op jit(solution)/shard_map/pallas_call | solution.py:313
  33.6 2.9 %all-to-all-done.1.scores_ref = f32[32,4,128]{2,1,0:T(4,128)S(1)} async-done(((f32[32,4,128]{2,1,0:T(4,128)}), f32[32,4,128]{2,1,0:T(4,128)S(1)}, u32[]{:S(2)}, u32[]{:S(2)}) %all-to-all-start.1) | async-done | bytes 65568 | tf_op jit(solution)/shard_map/all_to_all | solution.py:312
  36.5 1.3 %shard_map.81 = (f32[16,256]{1,0:T(8,128)S(1)}, f32[32,8,128]{2,1,0:T(8,128)S(1)}, f32[1,128]{1,0:T(1,128)S(1)}) custom-call(f32[32,4,128]{2,1,0:T(4,128)S(1)} %all-to-all-done.1.scores_ref, f32[32,32,128]{2,1,0:T(8,128)S(1)} %get-tuple-element.17.pairs_ref, bf16[2,256,256]{2,1,0:T(8,128)(2,1)S(1)} %get-tuple-element.18.query_ref), custom_call_target="tpu_custom_call" | custom-call | flops 134217728 | bytes 2097152 | tf_op jit(solution)/shard_map/pallas_call | solution.py:323
  37.9 0.5 %collective-permute-start.5 = (f32[16,256]{1,0:T(8,128)S(1)}, f32[16,256]{1,0:T(8,128)S(1)}, u32[]{:S(2)}, u32[]{:S(2)}) collective-permute-start(f32[16,256]{1,0:T(8,128)S(1)} %get-tuple-element.19), channel_id=1, source_target_pairs={{0,2},{1,3},{2,0},{3,1},{4,6},{5,7},{6,4},{7,5},{8,10},{9,11},{10,... | collective-permute-start | bytes 49160 | tf_op jit(solution)/shard_map/ppermute | solution.py:269
  38.4 1.7 %shard_map.82 = (f32[16,256]{1,0:T(8,128)S(1)}, f32[4]{0:T(128)}) custom-call(f32[32,8,128]{2,1,0:T(8,128)S(1)} %get-tuple-element.20.weight_ref, f32[1,128]{1,0:T(1,128)S(1)} %get-tuple-element.21.loss_ref, f32[32,32,128]{2,1,0:T(8,128)S(1)} %get-tuple-element.17.pairs_ref, bf16[2,256,256]{2,1,0:T(8,128)(2,1)S(1)} %get-tuple-element.18.query_ref), custom_call_target="tpu_custom_call" | custom-call | flops 134217728 | bytes 2097152 | tf_op jit(solution)/shard_map/pallas_call | solution.py:333
  40.1 1.6 %collective-permute-done.5 = f32[16,256]{1,0:T(8,128)S(1)} collective-permute-done((f32[16,256]{1,0:T(8,128)S(1)}, f32[16,256]{1,0:T(8,128)S(1)}, u32[]{:S(2)}, u32[]{:S(2)}) %collective-permute-start.5) | collective-permute-done | bytes 16416 | tf_op jit(solution)/shard_map/ppermute | solution.py:269
  41.7 0.6 %maximum_select_fusion = f32[16,512]{1,0:T(8,128)} fusion(f32[16,256]{1,0:T(8,128)S(1)} %get-tuple-element.22, f32[16,256]{1,0:T(8,128)S(1)} %collective-permute-done.5, pred[]{:T(512)S(6)} %eq.3), kind=kLoop, calls=%fused_computation | loop fusion | flops 24576 | bytes 65537 | tf_op jit(solution)/shard_map/jit(_where)/select_n | solution.py:343
Async XLA Ops:
  0.6 11.5 %copy-start = (f32[256,1024]{1,0:T(8,128)S(1)}, f32[256,1024]{1,0:T(8,128)}, u32[]{:S(2)}) copy-start(f32[256,1024]{1,0:T(8,128)} %book_ref.1) | copy-start | bytes 3145732
  2.6 20.8 %all-to-all-start = ((f32[32,25,1,128]{3,2,1,0:T(1,128)}), f32[32,25,1,128]{3,2,1,0:T(1,128)S(1)}, u32[]{:S(2)}, u32[]{:S(2)}) async-start(f32[32,25,1,128]{3,2,1,0:T(1,128)} %bitcast.5), calls=%async_computation | async-start | bytes 819200 | tf_op jit(solution)/shard_map/all_to_all | solution.py:295
  9.9 2.3 %collective-permute-start.1 = (f32[128,1024]{1,0:T(8,128)}, f32[128,1024]{1,0:T(8,128)S(1)}, u32[]{:S(2)}, u32[]{:S(2)}) collective-permute-start(f32[128,1024]{1,0:T(8,128)} %docs_ref.1), channel_id=1, source_target_pairs={{0,1},{1,0},{2,3},{3,2},{4,5},{5,4},{6,7},{7,6},{8,9},{9,8},{10,11... | collective-permute-start | bytes 1572872 | tf_op jit(solution)/shard_map/ppermute | solution.py:269
  10.2 2.0 %collective-permute-start = (s32[128,128]{1,0:T(8,128)}, s32[128,128]{1,0:T(8,128)S(1)}, u32[]{:S(2)}, u32[]{:S(2)}) collective-permute-start(s32[128,128]{1,0:T(8,128)} %codes_ref.1), channel_id=1, source_target_pairs={{0,1},{1,0},{2,3},{3,2},{4,5},{5,4},{6,7},{7,6},{8,9},{9,8},{10,11... | collective-permute-start | bytes 196616 | tf_op jit(solution)/shard_map/ppermute | solution.py:269
  12.2 1.0 %copy-start.1 = (f32[128,1024]{1,0:T(8,128)S(1)}, f32[128,1024]{1,0:T(8,128)}, u32[]{:S(2)}) copy-start(f32[128,1024]{1,0:T(8,128)} %docs_ref.1) | copy-start | bytes 1572868
  13.2 0.8 %copy-start.2 = (s32[128,128]{1,0:T(8,128)S(1)}, s32[128,128]{1,0:T(8,128)}, u32[]{:S(2)}) copy-start(s32[128,128]{1,0:T(8,128)} %codes_ref.1) | copy-start | bytes 196612
  24.7 8.5 %collective-permute-start.3 = (f32[800,128]{1,0:T(8,128)S(1)}, f32[800,128]{1,0:T(8,128)S(1)}, u32[]{:S(2)}, u32[]{:S(2)}) collective-permute-start(f32[800,128]{1,0:T(8,128)S(1)} %bitcast.3), channel_id=1, source_target_pairs={{0,1},{1,0},{2,3},{3,2},{4,5},{5,4},{6,7},{7,6},{8,9},{9,8},{10,11... | collective-permute-start | bytes 1228808 | tf_op jit(solution)/shard_map/ppermute | solution.py:269
  24.7 6.3 %collective-permute-start.2 = (f32[32,8,128]{2,1,0:T(8,128)S(1)}, f32[32,8,128]{2,1,0:T(8,128)S(1)}, u32[]{:S(2)}, u32[]{:S(2)}) collective-permute-start(f32[32,8,128]{2,1,0:T(8,128)S(1)} %get-tuple-element.16.codes_ref), channel_id=1, source_target_pairs={{0,4},{1,5},{2,6},{3,7},{4,0},{5,1},{6,2},{7,3},{8,12},{9,13},{10,... | collective-permute-start | bytes 393224 | tf_op jit(solution)/shard_map/ppermute | solution.py:269
  25.5 7.6 %collective-permute-start.4 = (f32[32,8,128]{2,1,0:T(8,128)S(1)}, f32[32,8,128]{2,1,0:T(8,128)S(1)}, u32[]{:S(2)}, u32[]{:S(2)}) collective-permute-start(f32[32,8,128]{2,1,0:T(8,128)S(1)} %get-tuple-element.16.codes_ref), channel_id=1, source_target_pairs={{0,5},{1,4},{2,7},{3,6},{4,1},{5,0},{6,3},{7,2},{8,13},{9,12},{10,... | collective-permute-start | bytes 393224 | tf_op jit(solution)/shard_map/ppermute | solution.py:269
  26.5 10.0 %all-to-all-start.1 = ((f32[32,4,128]{2,1,0:T(4,128)}), f32[32,4,128]{2,1,0:T(4,128)S(1)}, u32[]{:S(2)}, u32[]{:S(2)}) async-start(f32[32,4,128]{2,1,0:T(4,128)} %get-tuple-element.14), calls=%async_computation.1 | async-start | bytes 131072 | tf_op jit(solution)/shard_map/all_to_all | solution.py:312
  37.9 3.8 %collective-permute-start.5 = (f32[16,256]{1,0:T(8,128)S(1)}, f32[16,256]{1,0:T(8,128)S(1)}, u32[]{:S(2)}, u32[]{:S(2)}) collective-permute-start(f32[16,256]{1,0:T(8,128)S(1)} %get-tuple-element.19), channel_id=1, source_target_pairs={{0,2},{1,3},{2,0},{3,1},{4,6},{5,7},{6,4},{7,5},{8,10},{9,11},{10,... | collective-permute-start | bytes 49160 | tf_op jit(solution)/shard_map/ppermute | solution.py:269

commit v5 on v4

--- a/solution.py
+++ b/solution.py
@@ -19,7 +19,7 @@
 QN = 4
 HALF = TILES // 2
 BLOCK = 16
-TOGETHER = 4
+TOGETHER = 16
 ROWS = HALF * QN + SUB + 1
 
 
@@ -150,30 +150,28 @@
         codes_ref[p] = got_ref[first : first + SUB, :]
 
 
-def pair_kernel(got_ref, codes_ref, more_ref, other_ref, other_more_ref, out_ref, query_ref):
+def pair_kernel(got_ref, near_ref, z_ref, x_ref, both_ref, out_ref, query_ref):
     group, dev = place()
-    core, half = lax.rem(dev, 2), group * 2 + lax.div(lax.rem(dev, 4), 2)
+    across = lax.rem(lax.div(dev, 2), 2)
     own = lax.rem(lax.div(dev, 4), 2)
     asked = got_ref[pl.ds(ROWS - 1, C, stride=ROWS), :]
     asked = jnp.concatenate([asked, jnp.zeros((LANE - C, LANE), jnp.float32)], axis=0).T
     local = jnp.concatenate([asked[q * C : (q + 1) * C, :C] for q in range(QN)], axis=1)
     local = local.astype(jnp.int32)
-    for ref, tile in ((got_ref, core), (other_ref, 1 - core)):
-        first, second, _ = thirds(query_rows(ref, half * QN))
+    for tile in range(2):
+        first, second, _ = thirds(query_rows(got_ref, (group * 2 + tile) * QN))
         for rows in (slice(0, LANE), slice(LANE, 2 * LANE)):
             query_ref[tile, rows, :LANE] = first
             query_ref[tile, rows, LANE:] = second
     at = [
         pl.ds(pl.multiple_of(tile * SPT + part * SUB, SUB), SUB)
-        for tile in (core, 1 - core)
+        for tile in (across, 1 - across)
         for part in (own, 1 - own)
     ]
     for o in range(C):
         index = jnp.broadcast_to(local[o : o + 1, :], (SUB, LANE))
-        row = o * ROWS + HALF * QN
-        found = (codes_ref[o], more_ref[o], other_ref[row : row + SUB, :], other_more_ref[o])
-        for rows, value in zip(at, found):
-            out_ref[o, rows, :] = jnp.take_along_axis(value, index, axis=1)
+        for rows, ref in zip(at, (near_ref, z_ref, x_ref, both_ref)):
+            out_ref[o, rows, :] = jnp.take_along_axis(ref[o], index, axis=1)
 
 
 def log_parts(scores):
@@ -233,7 +231,7 @@
     share = soft - teacher
     for o in range(C):
         weight_ref[o] = jnp.broadcast_to(share[o : o + 1, :], (SUB, LANE))
-    block((dev ^ 2) * BLOCK, weight_ref, pairs_ref, query_ref, table, out_ref)
+    block((dev ^ 1) * BLOCK, weight_ref, pairs_ref, query_ref, table, out_ref)
 
 
 def here_kernel(weight_ref, loss_ref, pairs_ref, query_ref, out_ref, own_loss_ref, table):
@@ -307,8 +305,6 @@
     scores, codes = call(
         score_kernel, (f32(C, 4, LANE), f32(C, SUB, LANE)), 2, (), tuple(vmem(2)), 1 << 27, 1 << 21
     )(got, table)
-    more = by_xor(codes, 4, owners)
-    scores, after = lax.optimization_barrier((scores, got))
     all_scores = lax.all_to_all(scores, everyone, split_axis=0, concat_axis=0, tiled=True)
     pairs, columns = call(
         pair_kernel,
@@ -318,7 +314,7 @@
         tuple(vmem(2)),
         1 << 20,
         1 << 20,
-    )(after, codes, more, by_xor(after, 1, owners), by_xor(codes, 5, owners))
+    )(got, codes, *[by_xor(codes, bits, owners) for bits in (4, 2, 6)])
     built = [pltpu.VMEM((2 * SPT * BLOCK, 2 * LANE), jnp.bfloat16)]
     there, weight, losses = call(
         there_kernel,
@@ -329,7 +325,7 @@
         1 << 27,
         1 << 21,
     )(all_scores, pairs, columns)
-    far = by_xor(there, 2, owners)
+    far = by_xor(there, 1, owners)
     here, query_loss = call(
         here_kernel,
         (f32(BLOCK, 2 * LANE), f32(QN)),
@@ -339,9 +335,10 @@
         1 << 27,
         1 << 21,
     )(weight, losses, pairs, columns)
-    second = lax.rem(lax.div(lax.axis_index("dev"), 2), 2) == 1
-    gradient = jnp.where(
-        second, jnp.concatenate([far, here], 1), jnp.concatenate([here, far], 1)
+    odd = lax.rem(lax.axis_index("dev"), 2) == 1
+    even, later = jnp.where(odd, far, here), jnp.where(odd, here, far)
+    gradient = jnp.concatenate(
+        [even[:, :LANE], later[:, :LANE], even[:, LANE:], later[:, LANE:]], axis=1
     )
     return gradient, query_loss
 

time: 42.6 us -> 42.2 us (level)
  waiting for transfers between devices: 18.5 us -> 16.9 us
  starting transfers between devices: 12.8 us -> 14.1 us
    ppermute x6, waiting for transfers between devices: 7.34 us -> 4.34 us  [by_xor(): return lax.ppermute(value, 'dev', [(i, i ^ bits) for i in range(count)])]
    all_to_all x1, waiting for transfers between devices: 2.89 us -> 4.3 us  [shards_once(): lax.all_to_all(scores, everyone, split_axis=0, concat_axis=0, tiled=True)]
    ppermute x6, starting transfers between devices: 2.95 us -> 4.24 us  [by_xor(): return lax.ppermute(value, 'dev', [(i, i ^ bits) for i in range(count)])]
    concatenate x0 -> x1, other arithmetic: none -> 0.62 us  [shards_once(): jnp.concatenate([even[:, :LANE], later[:, :LANE], even[:, LANE:], later[:...]
    select_n x1, other arithmetic: 0.62 us -> 0.01 us  [shards_once(): even, later = (jnp.where(odd, far, here), jnp.where(odd, here, far))]
  transfers between devices with their start and end apart: 8 -> 8, of which waited for: 6 -> 6; matrix products, arithmetic and copies ran while one was open for 0% -> 0% of each run, Pallas kernels for 8% -> 7%
where the time goes in v5:
time: 42.2 us; the launch traced here: 41.9 us
  waiting for transfers between devices  16.9 us (40%)
  starting transfers between devices  14.1 us (33%)
  Pallas kernels  7.64 us (18%)
  local copies, waits for them, and re-layouts  1.89 us (4%)
  between operations  0.72 us (2%)
  other arithmetic  0.63 us (1%)
    all_to_all x1, waiting for transfers between devices, shards_once(): lax.all_to_all(sent.reshape(C, ROWS, 1, LANE), everyone, split_axis=0, co...  8.26 us
    all_to_all x1, starting transfers between devices, shards_once(): lax.all_to_all(sent.reshape(C, ROWS, 1, LANE), everyone, split_axis=0, co...  7.3 us
    ppermute x6, waiting for transfers between devices, by_xor(): return lax.ppermute(value, 'dev', [(i, i ^ bits) for i in range(count)])  4.34 us
    all_to_all x1, waiting for transfers between devices, shards_once(): lax.all_to_all(scores, everyone, split_axis=0, concat_axis=0, tiled=True)  4.3 us
    ppermute x6, starting transfers between devices, by_xor(): return lax.ppermute(value, 'dev', [(i, i ^ bits) for i in range(count)])  4.24 us
    all_to_all x1, starting transfers between devices, shards_once(): lax.all_to_all(scores, everyone, split_axis=0, concat_axis=0, tiled=True)  2.56 us
    pallas_call x1, Pallas kernels, shards_once(): call(pack_kernel, f32(C * ROWS, LANE), 4, [pltpu.VMEM((QN, D), jnp.float3...  1.93 us
    unnamed x6, local copies, waits for them, and re-layouts  1.88 us
  transfers between devices with their start and end apart: 8, of which 6 were waited for; matrix products, arithmetic and copies ran while one was open for 0% of the time, Pallas kernels for 7%

profile of v5, /device:TPU:0, one launch (start us, length us, event | category | flops | bytes accessed | tf_op | source)
XLA Modules:
  0.0 41.9 jit_solution(8745851588680818141)
XLA Ops:
  0.6 0.0 copy-start
  0.6 1.9 %shard_map.77 = f32[800,128]{1,0:T(8,128)} custom-call(f32[4,1024]{1,0:T(4,128)} %refs_0_.1, s32[128,128]{1,0:T(8,128)} %codes_ref.1, s32[4,32]{1,0:T(4,128)} %refs_2_.1, s32[4,32]{1,0:T(4,128)} %refs_3_.1), custom_call_target="tpu_custom_call" | custom-call | bytes 1048576 | tf_op jit(solution)/shard_map/pallas_call | solution.py:275
  2.6 7.3 %all-to-all-start = ((f32[32,25,1,128]{3,2,1,0:T(1,128)}), f32[32,25,1,128]{3,2,1,0:T(1,128)S(1)}, u32[]{:S(2)}, u32[]{:S(2)}) async-start(f32[32,25,1,128]{3,2,1,0:T(1,128)} %bitcast.4), calls=%async_computation | async-start | bytes 819200 | tf_op jit(solution)/shard_map/all_to_all | solution.py:293
  9.9 0.3 collective-permute-start.1
  10.2 0.3 collective-permute-start
  10.5 1.7 %collective-permute-done.other_ref = s32[128,128]{1,0:T(8,128)S(1)} collective-permute-done((s32[128,128]{1,0:T(8,128)}, s32[128,128]{1,0:T(8,128)S(1)}, u32[]{:S(2)}, u32[]{:S(2)}) %collective-permute-start) | collective-permute-done | bytes 65568 | tf_op jit(solution)/shard_map/ppermute | solution.py:267
  12.2 0.0 collective-permute-done.1.other_docs_ref
  12.2 0.0 copy-done
  12.2 0.0 copy-start.1
  12.2 1.0 %copy-done.1 = f32[128,1024]{1,0:T(8,128)S(1)} copy-done((f32[128,1024]{1,0:T(8,128)S(1)}, f32[128,1024]{1,0:T(8,128)}, u32[]{:S(2)}) %copy-start.1) | copy-done | bytes 524312
  13.2 0.0 copy-start.2
  13.2 0.8 %copy-done.2 = s32[128,128]{1,0:T(8,128)S(1)} copy-done((s32[128,128]{1,0:T(8,128)S(1)}, s32[128,128]{1,0:T(8,128)}, u32[]{:S(2)}) %copy-start.2) | copy-done | bytes 65560
  14.1 1.0 %shard_map.78.table_ref = bf16[3,512,512]{2,1,0:T(8,128)(2,1)S(1)} custom-call(s32[128,128]{1,0:T(8,128)S(1)} %copy-done.2, s32[128,128]{1,0:T(8,128)S(1)} %collective-permute-done.other_ref, f32[256,1024]{1,0:T(8,128)S(1)} %copy-done, f32[128,1024]{1,0:T(8,128)S(1)} %copy-done.1, f32[128,1024]{1,0:T(8,128)S(1)} %collective-permute-done.1.other_docs_ref), custom_call_target="tpu_custom_call" | custom-call | flops 4194304 | bytes 2097152 | tf_op jit(solution)/shard_map/pallas_call | solution.py:296
  15.1 8.3 %all-to-all-done = f32[32,25,1,128]{3,2,1,0:T(1,128)S(1)} async-done(((f32[32,25,1,128]{3,2,1,0:T(1,128)}), f32[32,25,1,128]{3,2,1,0:T(1,128)S(1)}, u32[]{:S(2)}, u32[]{:S(2)}) %all-to-all-start) | async-done | bytes 409632 | tf_op jit(solution)/shard_map/all_to_all | solution.py:293
  23.3 1.3 %shard_map.79 = (f32[32,4,128]{2,1,0:T(4,128)}, f32[32,8,128]{2,1,0:T(8,128)S(1)}) custom-call(f32[800,128]{1,0:T(8,128)S(1)} %bitcast.2, bf16[3,512,512]{2,1,0:T(8,128)(2,1)S(1)} %shard_map.78.table_ref), custom_call_target="tpu_custom_call" | custom-call | flops 134217728 | bytes 2097152 | tf_op jit(solution)/shard_map/pallas_call | solution.py:305
  24.7 0.9 %collective-permute-start.2 = (f32[32,8,128]{2,1,0:T(8,128)S(1)}, f32[32,8,128]{2,1,0:T(8,128)S(1)}, u32[]{:S(2)}, u32[]{:S(2)}) collective-permute-start(f32[32,8,128]{2,1,0:T(8,128)S(1)} %get-tuple-element.12.near_ref), channel_id=1, source_target_pairs={{0,4},{1,5},{2,6},{3,7},{4,0},{5,1},{6,2},{7,3},{8,12},{9,13},{10,... | collective-permute-start | bytes 393224 | tf_op jit(solution)/shard_map/ppermute | solution.py:267
  25.5 0.6 %collective-permute-start.3 = (f32[32,8,128]{2,1,0:T(8,128)S(1)}, f32[32,8,128]{2,1,0:T(8,128)S(1)}, u32[]{:S(2)}, u32[]{:S(2)}) collective-permute-start(f32[32,8,128]{2,1,0:T(8,128)S(1)} %get-tuple-element.12.near_ref), channel_id=1, source_target_pairs={{0,2},{1,3},{2,0},{3,1},{4,6},{5,7},{6,4},{7,5},{8,10},{9,11},{10,... | collective-permute-start | bytes 393224 | tf_op jit(solution)/shard_map/ppermute | solution.py:267
  26.2 2.0 %collective-permute-start.4 = (f32[32,8,128]{2,1,0:T(8,128)S(1)}, f32[32,8,128]{2,1,0:T(8,128)S(1)}, u32[]{:S(2)}, u32[]{:S(2)}) collective-permute-start(f32[32,8,128]{2,1,0:T(8,128)S(1)} %get-tuple-element.12.near_ref), channel_id=1, source_target_pairs={{0,6},{1,7},{2,4},{3,5},{4,2},{5,3},{6,0},{7,1},{8,14},{9,15},{10,... | collective-permute-start | bytes 393224 | tf_op jit(solution)/shard_map/ppermute | solution.py:267
  28.2 2.6 %all-to-all-start.1 = ((f32[32,4,128]{2,1,0:T(4,128)}), f32[32,4,128]{2,1,0:T(4,128)S(1)}, u32[]{:S(2)}, u32[]{:S(2)}) async-start(f32[32,4,128]{2,1,0:T(4,128)} %get-tuple-element.11), calls=%async_computation.1 | async-start | bytes 131072 | tf_op jit(solution)/shard_map/all_to_all | solution.py:308
  30.7 0.1 collective-permute-done.2.z_ref
  30.8 1.0 %collective-permute-done.3.x_ref = f32[32,8,128]{2,1,0:T(8,128)S(1)} collective-permute-done((f32[32,8,128]{2,1,0:T(8,128)S(1)}, f32[32,8,128]{2,1,0:T(8,128)S(1)}, u32[]{:S(2)}, u32[]{:S(2)}) %collective-permute-start.3) | collective-permute-done | bytes 131104 | tf_op jit(solution)/shard_map/ppermute | solution.py:267
  31.8 1.6 %collective-permute-done.4.both_ref = f32[32,8,128]{2,1,0:T(8,128)S(1)} collective-permute-done((f32[32,8,128]{2,1,0:T(8,128)S(1)}, f32[32,8,128]{2,1,0:T(8,128)S(1)}, u32[]{:S(2)}, u32[]{:S(2)}) %collective-permute-start.4) | collective-permute-done | bytes 131104 | tf_op jit(solution)/shard_map/ppermute | solution.py:267
  33.4 0.5 %shard_map.80 = (f32[32,32,128]{2,1,0:T(8,128)S(1)}, bf16[2,256,256]{2,1,0:T(8,128)(2,1)S(1)}) custom-call(f32[800,128]{1,0:T(8,128)S(1)} %bitcast.3, f32[32,8,128]{2,1,0:T(8,128)S(1)} %get-tuple-element.12.near_ref, f32[32,8,128]{2,1,0:T(8,128)S(1)} %collective-permute-done.2.z_ref, f32[32,8,128]{2,1,0:T(8,128)S(1)} %collective-permute-done.3.x_ref, ...), custom_call_target="tpu_custom_call" | custom-call | flops 1048576 | bytes 1048576 | tf_op jit(solution)/shard_map/pallas_call | solution.py:309
  33.8 4.3 %all-to-all-done.1.scores_ref = f32[32,4,128]{2,1,0:T(4,128)S(1)} async-done(((f32[32,4,128]{2,1,0:T(4,128)}), f32[32,4,128]{2,1,0:T(4,128)S(1)}, u32[]{:S(2)}, u32[]{:S(2)}) %all-to-all-start.1) | async-done | bytes 65568 | tf_op jit(solution)/shard_map/all_to_all | solution.py:308
  38.1 1.3 %shard_map.81 = (f32[16,256]{1,0:T(8,128)S(1)}, f32[32,8,128]{2,1,0:T(8,128)S(1)}, f32[1,128]{1,0:T(1,128)S(1)}) custom-call(f32[32,4,128]{2,1,0:T(4,128)S(1)} %all-to-all-done.1.scores_ref, f32[32,32,128]{2,1,0:T(8,128)S(1)} %get-tuple-element.13.pairs_ref, bf16[2,256,256]{2,1,0:T(8,128)(2,1)S(1)} %get-tuple-element.14.query_ref), custom_call_target="tpu_custom_call" | custom-call | flops 134217728 | bytes 2097152 | tf_op jit(solution)/shard_map/pallas_call | solution.py:319
  39.4 0.2 collective-permute-start.5
  39.6 1.6 %shard_map.82 = (f32[16,256]{1,0:T(8,128)S(1)}, f32[4]{0:T(128)}) custom-call(f32[32,8,128]{2,1,0:T(8,128)S(1)} %get-tuple-element.16.weight_ref, f32[1,128]{1,0:T(1,128)S(1)} %get-tuple-element.17.loss_ref, f32[32,32,128]{2,1,0:T(8,128)S(1)} %get-tuple-element.13.pairs_ref, bf16[2,256,256]{2,1,0:T(8,128)(2,1)S(1)} %get-tuple-element.14.query_ref), custom_call_target="tpu_custom_call" | custom-call | flops 134217728 | bytes 2097152 | tf_op jit(solution)/shard_map/pallas_call | solution.py:329
  41.2 0.0 collective-permute-done.5
  41.3 0.6 %pad_maximum_fusion = f32[16,512]{1,0:T(8,128)} fusion(f32[16,128]{1,0:T(8,128)S(1)} %get-tuple-element.26, f32[16,128]{1,0:T(8,128)S(1)} %get-tuple-element.23, f32[16,128]{1,0:T(8,128)S(1)} %get-tuple-element.27, f32[16,128]{1,0:T(8,128)S(1)} %get-tuple-element.22), kind=kLoop, calls=%fused_computation | loop fusion | flops 24576 | bytes 65536 | tf_op jit(solution)/shard_map/concatenate | solution.py:340
  (2 shorter events, 0.0 us)
Async XLA Ops:
  0.6 11.5 %copy-start = (f32[256,1024]{1,0:T(8,128)S(1)}, f32[256,1024]{1,0:T(8,128)}, u32[]{:S(2)}) copy-start(f32[256,1024]{1,0:T(8,128)} %book_ref.1) | copy-start | bytes 3145732
  2.6 20.8 %all-to-all-start = ((f32[32,25,1,128]{3,2,1,0:T(1,128)}), f32[32,25,1,128]{3,2,1,0:T(1,128)S(1)}, u32[]{:S(2)}, u32[]{:S(2)}) async-start(f32[32,25,1,128]{3,2,1,0:T(1,128)} %bitcast.4), calls=%async_computation | async-start | bytes 819200 | tf_op jit(solution)/shard_map/all_to_all | solution.py:293
  9.9 2.3 %collective-permute-start.1 = (f32[128,1024]{1,0:T(8,128)}, f32[128,1024]{1,0:T(8,128)S(1)}, u32[]{:S(2)}, u32[]{:S(2)}) collective-permute-start(f32[128,1024]{1,0:T(8,128)} %docs_ref.1), channel_id=1, source_target_pairs={{0,1},{1,0},{2,3},{3,2},{4,5},{5,4},{6,7},{7,6},{8,9},{9,8},{10,11... | collective-permute-start | bytes 1572872 | tf_op jit(solution)/shard_map/ppermute | solution.py:267
  10.2 2.0 %collective-permute-start = (s32[128,128]{1,0:T(8,128)}, s32[128,128]{1,0:T(8,128)S(1)}, u32[]{:S(2)}, u32[]{:S(2)}) collective-permute-start(s32[128,128]{1,0:T(8,128)} %codes_ref.1), channel_id=1, source_target_pairs={{0,1},{1,0},{2,3},{3,2},{4,5},{5,4},{6,7},{7,6},{8,9},{9,8},{10,11... | collective-permute-start | bytes 196616 | tf_op jit(solution)/shard_map/ppermute | solution.py:267
  12.2 1.0 %copy-start.1 = (f32[128,1024]{1,0:T(8,128)S(1)}, f32[128,1024]{1,0:T(8,128)}, u32[]{:S(2)}) copy-start(f32[128,1024]{1,0:T(8,128)} %docs_ref.1) | copy-start | bytes 1572868
  13.2 0.8 %copy-start.2 = (s32[128,128]{1,0:T(8,128)S(1)}, s32[128,128]{1,0:T(8,128)}, u32[]{:S(2)}) copy-start(s32[128,128]{1,0:T(8,128)} %codes_ref.1) | copy-start | bytes 196612
  24.7 6.2 %collective-permute-start.2 = (f32[32,8,128]{2,1,0:T(8,128)S(1)}, f32[32,8,128]{2,1,0:T(8,128)S(1)}, u32[]{:S(2)}, u32[]{:S(2)}) collective-permute-start(f32[32,8,128]{2,1,0:T(8,128)S(1)} %get-tuple-element.12.near_ref), channel_id=1, source_target_pairs={{0,4},{1,5},{2,6},{3,7},{4,0},{5,1},{6,2},{7,3},{8,12},{9,13},{10,... | collective-permute-start | bytes 393224 | tf_op jit(solution)/shard_map/ppermute | solution.py:267
  25.5 6.3 %collective-permute-start.3 = (f32[32,8,128]{2,1,0:T(8,128)S(1)}, f32[32,8,128]{2,1,0:T(8,128)S(1)}, u32[]{:S(2)}, u32[]{:S(2)}) collective-permute-start(f32[32,8,128]{2,1,0:T(8,128)S(1)} %get-tuple-element.12.near_ref), channel_id=1, source_target_pairs={{0,2},{1,3},{2,0},{3,1},{4,6},{5,7},{6,4},{7,5},{8,10},{9,11},{10,... | collective-permute-start | bytes 393224 | tf_op jit(solution)/shard_map/ppermute | solution.py:267
  26.2 7.2 %collective-permute-start.4 = (f32[32,8,128]{2,1,0:T(8,128)S(1)}, f32[32,8,128]{2,1,0:T(8,128)S(1)}, u32[]{:S(2)}, u32[]{:S(2)}) collective-permute-start(f32[32,8,128]{2,1,0:T(8,128)S(1)} %get-tuple-element.12.near_ref), channel_id=1, source_target_pairs={{0,6},{1,7},{2,4},{3,5},{4,2},{5,3},{6,0},{7,1},{8,14},{9,15},{10,... | collective-permute-start | bytes 393224 | tf_op jit(solution)/shard_map/ppermute | solution.py:267
  28.2 10.0 %all-to-all-start.1 = ((f32[32,4,128]{2,1,0:T(4,128)}), f32[32,4,128]{2,1,0:T(4,128)S(1)}, u32[]{:S(2)}, u32[]{:S(2)}) async-start(f32[32,4,128]{2,1,0:T(4,128)} %get-tuple-element.11), calls=%async_computation.1 | async-start | bytes 131072 | tf_op jit(solution)/shard_map/all_to_all | solution.py:308
  39.4 1.8 %collective-permute-start.5 = (f32[16,256]{1,0:T(8,128)S(1)}, f32[16,256]{1,0:T(8,128)S(1)}, u32[]{:S(2)}, u32[]{:S(2)}) collective-permute-start(f32[16,256]{1,0:T(8,128)S(1)} %get-tuple-element.15), channel_id=1, source_target_pairs={{0,1},{1,0},{2,3},{3,2},{4,5},{5,4},{6,7},{7,6},{8,9},{9,8},{10,11... | collective-permute-start | bytes 49160 | tf_op jit(solution)/shard_map/ppermute | solution.py:267

commit v6 on v5

--- a/solution.py
+++ b/solution.py
@@ -236,10 +236,10 @@
 
 def here_kernel(weight_ref, loss_ref, pairs_ref, query_ref, out_ref, own_loss_ref, table):
     group, dev = place()
-    lanes = iota((1, LANE), 1)
+    mine = iota((SUB, LANE), 1) == iota((SUB, LANE), 0) * C + (group * 16 + dev)
+    picked = jnp.sum(jnp.where(mine, loss_ref[...], 0.0), axis=1, keepdims=True)
     for q in range(QN):
-        mine = lanes == q * C + group * 16 + dev
-        own_loss_ref[q] = jnp.sum(jnp.where(mine, loss_ref[...], 0.0))
+        own_loss_ref[q] = picked[q, 0]
     block(lax.axis_index("dev") * BLOCK, weight_ref, pairs_ref, query_ref, table, out_ref)
 
 

time: 42.2 us -> 42.2 us (level)
  no operation moved by 1% of the time
where the time goes in v6:
time: 42.2 us; the launch traced here: 41.9 us
  waiting for transfers between devices  16.9 us (40%)
  starting transfers between devices  14.1 us (33%)
  Pallas kernels  7.63 us (18%)
  local copies, waits for them, and re-layouts  1.89 us (4%)
  between operations  0.72 us (2%)
  other arithmetic  0.63 us (1%)
    all_to_all x1, waiting for transfers between devices, shards_once(): lax.all_to_all(sent.reshape(C, ROWS, 1, LANE), everyone, split_axis=0, co...  8.26 us
    all_to_all x1, starting transfers between devices, shards_once(): lax.all_to_all(sent.reshape(C, ROWS, 1, LANE), everyone, split_axis=0, co...  7.3 us
    ppermute x6, waiting for transfers between devices, by_xor(): return lax.ppermute(value, 'dev', [(i, i ^ bits) for i in range(count)])  4.34 us
    all_to_all x1, waiting for transfers between devices, shards_once(): lax.all_to_all(scores, everyone, split_axis=0, concat_axis=0, tiled=True)  4.3 us
    ppermute x6, starting transfers between devices, by_xor(): return lax.ppermute(value, 'dev', [(i, i ^ bits) for i in range(count)])  4.24 us
    all_to_all x1, starting transfers between devices, shards_once(): lax.all_to_all(scores, everyone, split_axis=0, concat_axis=0, tiled=True)  2.56 us
    pallas_call x1, Pallas kernels, shards_once(): call(pack_kernel, f32(C * ROWS, LANE), 4, [pltpu.VMEM((QN, D), jnp.float3...  1.93 us
    unnamed x6, local copies, waits for them, and re-layouts  1.88 us
  transfers between devices with their start and end apart: 8, of which 6 were waited for; matrix products, arithmetic and copies ran while one was open for 0% of the time, Pallas kernels for 7%

profile of v6, /device:TPU:0, one launch (start us, length us, event | category | flops | bytes accessed | tf_op | source)
XLA Modules:
  0.0 41.9 jit_solution(10238514253098866093)
XLA Ops:
  0.6 0.0 copy-start
  0.6 1.9 %shard_map.77 = f32[800,128]{1,0:T(8,128)} custom-call(f32[4,1024]{1,0:T(4,128)} %refs_0_.1, s32[128,128]{1,0:T(8,128)} %codes_ref.1, s32[4,32]{1,0:T(4,128)} %refs_2_.1, s32[4,32]{1,0:T(4,128)} %refs_3_.1), custom_call_target="tpu_custom_call" | custom-call | bytes 1048576 | tf_op jit(solution)/shard_map/pallas_call | solution.py:275
  2.6 7.3 %all-to-all-start = ((f32[32,25,1,128]{3,2,1,0:T(1,128)}), f32[32,25,1,128]{3,2,1,0:T(1,128)S(1)}, u32[]{:S(2)}, u32[]{:S(2)}) async-start(f32[32,25,1,128]{3,2,1,0:T(1,128)} %bitcast.4), calls=%async_computation | async-start | bytes 819200 | tf_op jit(solution)/shard_map/all_to_all | solution.py:293
  9.9 0.3 collective-permute-start.1
  10.2 0.3 collective-permute-start
  10.5 1.7 %collective-permute-done.other_ref = s32[128,128]{1,0:T(8,128)S(1)} collective-permute-done((s32[128,128]{1,0:T(8,128)}, s32[128,128]{1,0:T(8,128)S(1)}, u32[]{:S(2)}, u32[]{:S(2)}) %collective-permute-start) | collective-permute-done | bytes 65568 | tf_op jit(solution)/shard_map/ppermute | solution.py:267
  12.2 0.0 collective-permute-done.1.other_docs_ref
  12.2 0.0 copy-done
  12.2 0.0 copy-start.1
  12.2 1.0 %copy-done.1 = f32[128,1024]{1,0:T(8,128)S(1)} copy-done((f32[128,1024]{1,0:T(8,128)S(1)}, f32[128,1024]{1,0:T(8,128)}, u32[]{:S(2)}) %copy-start.1) | copy-done | bytes 524312
  13.2 0.0 copy-start.2
  13.2 0.8 %copy-done.2 = s32[128,128]{1,0:T(8,128)S(1)} copy-done((s32[128,128]{1,0:T(8,128)S(1)}, s32[128,128]{1,0:T(8,128)}, u32[]{:S(2)}) %copy-start.2) | copy-done | bytes 65560
  14.1 1.0 %shard_map.78.table_ref = bf16[3,512,512]{2,1,0:T(8,128)(2,1)S(1)} custom-call(s32[128,128]{1,0:T(8,128)S(1)} %copy-done.2, s32[128,128]{1,0:T(8,128)S(1)} %collective-permute-done.other_ref, f32[256,1024]{1,0:T(8,128)S(1)} %copy-done, f32[128,1024]{1,0:T(8,128)S(1)} %copy-done.1, f32[128,1024]{1,0:T(8,128)S(1)} %collective-permute-done.1.other_docs_ref), custom_call_target="tpu_custom_call" | custom-call | flops 4194304 | bytes 2097152 | tf_op jit(solution)/shard_map/pallas_call | solution.py:296
  15.1 8.3 %all-to-all-done = f32[32,25,1,128]{3,2,1,0:T(1,128)S(1)} async-done(((f32[32,25,1,128]{3,2,1,0:T(1,128)}), f32[32,25,1,128]{3,2,1,0:T(1,128)S(1)}, u32[]{:S(2)}, u32[]{:S(2)}) %all-to-all-start) | async-done | bytes 409632 | tf_op jit(solution)/shard_map/all_to_all | solution.py:293
  23.3 1.3 %shard_map.79 = (f32[32,4,128]{2,1,0:T(4,128)}, f32[32,8,128]{2,1,0:T(8,128)S(1)}) custom-call(f32[800,128]{1,0:T(8,128)S(1)} %bitcast.2, bf16[3,512,512]{2,1,0:T(8,128)(2,1)S(1)} %shard_map.78.table_ref), custom_call_target="tpu_custom_call" | custom-call | flops 134217728 | bytes 2097152 | tf_op jit(solution)/shard_map/pallas_call | solution.py:305
  24.7 0.9 %collective-permute-start.2 = (f32[32,8,128]{2,1,0:T(8,128)S(1)}, f32[32,8,128]{2,1,0:T(8,128)S(1)}, u32[]{:S(2)}, u32[]{:S(2)}) collective-permute-start(f32[32,8,128]{2,1,0:T(8,128)S(1)} %get-tuple-element.12.near_ref), channel_id=1, source_target_pairs={{0,4},{1,5},{2,6},{3,7},{4,0},{5,1},{6,2},{7,3},{8,12},{9,13},{10,... | collective-permute-start | bytes 393224 | tf_op jit(solution)/shard_map/ppermute | solution.py:267
  25.5 0.6 %collective-permute-start.3 = (f32[32,8,128]{2,1,0:T(8,128)S(1)}, f32[32,8,128]{2,1,0:T(8,128)S(1)}, u32[]{:S(2)}, u32[]{:S(2)}) collective-permute-start(f32[32,8,128]{2,1,0:T(8,128)S(1)} %get-tuple-element.12.near_ref), channel_id=1, source_target_pairs={{0,2},{1,3},{2,0},{3,1},{4,6},{5,7},{6,4},{7,5},{8,10},{9,11},{10,... | collective-permute-start | bytes 393224 | tf_op jit(solution)/shard_map/ppermute | solution.py:267
  26.2 2.0 %collective-permute-start.4 = (f32[32,8,128]{2,1,0:T(8,128)S(1)}, f32[32,8,128]{2,1,0:T(8,128)S(1)}, u32[]{:S(2)}, u32[]{:S(2)}) collective-permute-start(f32[32,8,128]{2,1,0:T(8,128)S(1)} %get-tuple-element.12.near_ref), channel_id=1, source_target_pairs={{0,6},{1,7},{2,4},{3,5},{4,2},{5,3},{6,0},{7,1},{8,14},{9,15},{10,... | collective-permute-start | bytes 393224 | tf_op jit(solution)/shard_map/ppermute | solution.py:267
  28.2 2.6 %all-to-all-start.1 = ((f32[32,4,128]{2,1,0:T(4,128)}), f32[32,4,128]{2,1,0:T(4,128)S(1)}, u32[]{:S(2)}, u32[]{:S(2)}) async-start(f32[32,4,128]{2,1,0:T(4,128)} %get-tuple-element.11), calls=%async_computation.1 | async-start | bytes 131072 | tf_op jit(solution)/shard_map/all_to_all | solution.py:308
  30.7 0.1 collective-permute-done.2.z_ref
  30.8 1.0 %collective-permute-done.3.x_ref = f32[32,8,128]{2,1,0:T(8,128)S(1)} collective-permute-done((f32[32,8,128]{2,1,0:T(8,128)S(1)}, f32[32,8,128]{2,1,0:T(8,128)S(1)}, u32[]{:S(2)}, u32[]{:S(2)}) %collective-permute-start.3) | collective-permute-done | bytes 131104 | tf_op jit(solution)/shard_map/ppermute | solution.py:267
  31.8 1.6 %collective-permute-done.4.both_ref = f32[32,8,128]{2,1,0:T(8,128)S(1)} collective-permute-done((f32[32,8,128]{2,1,0:T(8,128)S(1)}, f32[32,8,128]{2,1,0:T(8,128)S(1)}, u32[]{:S(2)}, u32[]{:S(2)}) %collective-permute-start.4) | collective-permute-done | bytes 131104 | tf_op jit(solution)/shard_map/ppermute | solution.py:267
  33.4 0.5 %shard_map.80 = (f32[32,32,128]{2,1,0:T(8,128)S(1)}, bf16[2,256,256]{2,1,0:T(8,128)(2,1)S(1)}) custom-call(f32[800,128]{1,0:T(8,128)S(1)} %bitcast.3, f32[32,8,128]{2,1,0:T(8,128)S(1)} %get-tuple-element.12.near_ref, f32[32,8,128]{2,1,0:T(8,128)S(1)} %collective-permute-done.2.z_ref, f32[32,8,128]{2,1,0:T(8,128)S(1)} %collective-permute-done.3.x_ref, ...), custom_call_target="tpu_custom_call" | custom-call | flops 1048576 | bytes 1048576 | tf_op jit(solution)/shard_map/pallas_call | solution.py:309
  33.8 4.3 %all-to-all-done.1.scores_ref = f32[32,4,128]{2,1,0:T(4,128)S(1)} async-done(((f32[32,4,128]{2,1,0:T(4,128)}), f32[32,4,128]{2,1,0:T(4,128)S(1)}, u32[]{:S(2)}, u32[]{:S(2)}) %all-to-all-start.1) | async-done | bytes 65568 | tf_op jit(solution)/shard_map/all_to_all | solution.py:308
  38.1 1.3 %shard_map.81 = (f32[16,256]{1,0:T(8,128)S(1)}, f32[32,8,128]{2,1,0:T(8,128)S(1)}, f32[1,128]{1,0:T(1,128)S(1)}) custom-call(f32[32,4,128]{2,1,0:T(4,128)S(1)} %all-to-all-done.1.scores_ref, f32[32,32,128]{2,1,0:T(8,128)S(1)} %get-tuple-element.13.pairs_ref, bf16[2,256,256]{2,1,0:T(8,128)(2,1)S(1)} %get-tuple-element.14.query_ref), custom_call_target="tpu_custom_call" | custom-call | flops 134217728 | bytes 2097152 | tf_op jit(solution)/shard_map/pallas_call | solution.py:319
  39.4 0.2 collective-permute-start.5
  39.6 1.6 %shard_map.82 = (f32[16,256]{1,0:T(8,128)S(1)}, f32[4]{0:T(128)}) custom-call(f32[32,8,128]{2,1,0:T(8,128)S(1)} %get-tuple-element.16.weight_ref, f32[1,128]{1,0:T(1,128)S(1)} %get-tuple-element.17.loss_ref, f32[32,32,128]{2,1,0:T(8,128)S(1)} %get-tuple-element.13.pairs_ref, bf16[2,256,256]{2,1,0:T(8,128)(2,1)S(1)} %get-tuple-element.14.query_ref), custom_call_target="tpu_custom_call" | custom-call | flops 134217728 | bytes 2097152 | tf_op jit(solution)/shard_map/pallas_call | solution.py:329
  41.2 0.0 collective-permute-done.5
  41.3 0.6 %pad_maximum_fusion = f32[16,512]{1,0:T(8,128)} fusion(f32[16,128]{1,0:T(8,128)S(1)} %get-tuple-element.26, f32[16,128]{1,0:T(8,128)S(1)} %get-tuple-element.23, f32[16,128]{1,0:T(8,128)S(1)} %get-tuple-element.27, f32[16,128]{1,0:T(8,128)S(1)} %get-tuple-element.22), kind=kLoop, calls=%fused_computation | loop fusion | flops 24576 | bytes 65536 | tf_op jit(solution)/shard_map/concatenate | solution.py:340
  (2 shorter events, 0.0 us)
Async XLA Ops:
  0.6 11.5 %copy-start = (f32[256,1024]{1,0:T(8,128)S(1)}, f32[256,1024]{1,0:T(8,128)}, u32[]{:S(2)}) copy-start(f32[256,1024]{1,0:T(8,128)} %book_ref.1) | copy-start | bytes 3145732
  2.6 20.8 %all-to-all-start = ((f32[32,25,1,128]{3,2,1,0:T(1,128)}), f32[32,25,1,128]{3,2,1,0:T(1,128)S(1)}, u32[]{:S(2)}, u32[]{:S(2)}) async-start(f32[32,25,1,128]{3,2,1,0:T(1,128)} %bitcast.4), calls=%async_computation | async-start | bytes 819200 | tf_op jit(solution)/shard_map/all_to_all | solution.py:293
  9.9 2.3 %collective-permute-start.1 = (f32[128,1024]{1,0:T(8,128)}, f32[128,1024]{1,0:T(8,128)S(1)}, u32[]{:S(2)}, u32[]{:S(2)}) collective-permute-start(f32[128,1024]{1,0:T(8,128)} %docs_ref.1), channel_id=1, source_target_pairs={{0,1},{1,0},{2,3},{3,2},{4,5},{5,4},{6,7},{7,6},{8,9},{9,8},{10,11... | collective-permute-start | bytes 1572872 | tf_op jit(solution)/shard_map/ppermute | solution.py:267
  10.2 2.0 %collective-permute-start = (s32[128,128]{1,0:T(8,128)}, s32[128,128]{1,0:T(8,128)S(1)}, u32[]{:S(2)}, u32[]{:S(2)}) collective-permute-start(s32[128,128]{1,0:T(8,128)} %codes_ref.1), channel_id=1, source_target_pairs={{0,1},{1,0},{2,3},{3,2},{4,5},{5,4},{6,7},{7,6},{8,9},{9,8},{10,11... | collective-permute-start | bytes 196616 | tf_op jit(solution)/shard_map/ppermute | solution.py:267
  12.2 1.0 %copy-start.1 = (f32[128,1024]{1,0:T(8,128)S(1)}, f32[128,1024]{1,0:T(8,128)}, u32[]{:S(2)}) copy-start(f32[128,1024]{1,0:T(8,128)} %docs_ref.1) | copy-start | bytes 1572868
  13.2 0.8 %copy-start.2 = (s32[128,128]{1,0:T(8,128)S(1)}, s32[128,128]{1,0:T(8,128)}, u32[]{:S(2)}) copy-start(s32[128,128]{1,0:T(8,128)} %codes_ref.1) | copy-start | bytes 196612
  24.7 6.2 %collective-permute-start.2 = (f32[32,8,128]{2,1,0:T(8,128)S(1)}, f32[32,8,128]{2,1,0:T(8,128)S(1)}, u32[]{:S(2)}, u32[]{:S(2)}) collective-permute-start(f32[32,8,128]{2,1,0:T(8,128)S(1)} %get-tuple-element.12.near_ref), channel_id=1, source_target_pairs={{0,4},{1,5},{2,6},{3,7},{4,0},{5,1},{6,2},{7,3},{8,12},{9,13},{10,... | collective-permute-start | bytes 393224 | tf_op jit(solution)/shard_map/ppermute | solution.py:267
  25.5 6.3 %collective-permute-start.3 = (f32[32,8,128]{2,1,0:T(8,128)S(1)}, f32[32,8,128]{2,1,0:T(8,128)S(1)}, u32[]{:S(2)}, u32[]{:S(2)}) collective-permute-start(f32[32,8,128]{2,1,0:T(8,128)S(1)} %get-tuple-element.12.near_ref), channel_id=1, source_target_pairs={{0,2},{1,3},{2,0},{3,1},{4,6},{5,7},{6,4},{7,5},{8,10},{9,11},{10,... | collective-permute-start | bytes 393224 | tf_op jit(solution)/shard_map/ppermute | solution.py:267
  26.2 7.2 %collective-permute-start.4 = (f32[32,8,128]{2,1,0:T(8,128)S(1)}, f32[32,8,128]{2,1,0:T(8,128)S(1)}, u32[]{:S(2)}, u32[]{:S(2)}) collective-permute-start(f32[32,8,128]{2,1,0:T(8,128)S(1)} %get-tuple-element.12.near_ref), channel_id=1, source_target_pairs={{0,6},{1,7},{2,4},{3,5},{4,2},{5,3},{6,0},{7,1},{8,14},{9,15},{10,... | collective-permute-start | bytes 393224 | tf_op jit(solution)/shard_map/ppermute | solution.py:267
  28.2 10.0 %all-to-all-start.1 = ((f32[32,4,128]{2,1,0:T(4,128)}), f32[32,4,128]{2,1,0:T(4,128)S(1)}, u32[]{:S(2)}, u32[]{:S(2)}) async-start(f32[32,4,128]{2,1,0:T(4,128)} %get-tuple-element.11), calls=%async_computation.1 | async-start | bytes 131072 | tf_op jit(solution)/shard_map/all_to_all | solution.py:308
  39.4 1.8 %collective-permute-start.5 = (f32[16,256]{1,0:T(8,128)S(1)}, f32[16,256]{1,0:T(8,128)S(1)}, u32[]{:S(2)}, u32[]{:S(2)}) collective-permute-start(f32[16,256]{1,0:T(8,128)S(1)} %get-tuple-element.15), channel_id=1, source_target_pairs={{0,1},{1,0},{2,3},{3,2},{4,5},{5,4},{6,7},{7,6},{8,9},{9,8},{10,11... | collective-permute-start | bytes 49160 | tf_op jit(solution)/shard_map/ppermute | solution.py:267
